TPU v7x, 512 devices: a whole 4x4x16 slice. The times are simulated.
512 devices in a mesh: frow: 16 (over z_lo, y), fcol: 32 (over z_hi, x, core).
Axes of the slice: x: 4, y: 4, z: 16 (z_hi: 4, z_lo: 4; z = z_hi * 4 + z_lo), core: 2. Of those that a mesh axis runs over, the one named last changes fastest.
Arguments:
- vis: float32 [2, 131072], P(None, ('frow', 'fcol')), may hold values from -6 to 6
- station_pairs: int32 [2, 131072], P(None, ('frow', 'fcol')), may hold values from 0 to 511
- visibility_time_slot: int32 [131072], P(('frow', 'fcol')), may hold values from 0 to 15
- station_u_cells: int32 [512], replicated, may hold values from -4096 to 4095
- station_v_cells: int32 [512], replicated, may hold values from -4096 to 4095
- facet_station_gains: float32 [16, 32, 2, 8192], P('frow', 'fcol'), may hold values from -6 to 6
- holder_device_order: int32 [512], replicated, may hold values from 0 to 511, each once
Outputs:
- image: float32 [16384, 16384], P('frow', 'fcol')
Inputs may be any that keep to these rules, and one draw needn't show every extreme that they name: `holder_device_order`: a permutation; its first 4 entries name distinct devices.
All inputs are finite; a program needn't handle non-finite values.
Results may differ from a plain program's by a relative error of at most 0.0037.
Values sent between devices are 32-bit elements; how exact they have to be, the bound alone decides.
A program may use at most 64 MiB of HBM per device.

v0:
```python
import math

import jax
import jax.numpy as jnp
from jax import lax
from jax.sharding import PartitionSpec as P

R = 1024
C = 512
M = 64
NT = 16
NBLK = 4


def extended_2(x, sides, width):
    for axis, dim in sides:
        size, length = (lax.axis_size(axis), x.shape[dim])
        up = [(i, (i + 1) % size) for i in range(size - 1)]
        down = [(j, i) for i, j in up]
        last = lax.slice_in_dim(x, length - width, length, axis=dim)
        leading = lax.slice_in_dim(x, 0, width, axis=dim)
        before = lax.ppermute(last, axis, up)
        after = lax.ppermute(leading, axis, down)
        x = jnp.concatenate([before, x, after], axis=dim)
    return x


def broadcast(value, axis, source):
    kept = jnp.where(lax.axis_index(axis) == source, value, 0).astype(value.dtype)
    return lax.psum(kept, axis)


def taper_line(length):
    index = jnp.arange(length + 2 * M, dtype=jnp.int32).astype(jnp.float32)
    rising = (index + 0.5) / (2.0 * M)
    falling = (length + 2 * M - index - 0.5) / (2.0 * M)
    return jnp.minimum(jnp.minimum(rising, falling), 1.0)


def phase_angles(freq, pixels, modulus):
    cells = jnp.mod(freq, modulus)[None, :] * jnp.mod(pixels, modulus)[:, None] % modulus
    return cells.astype(jnp.float32) * (2.0 * math.pi / modulus)


def block_weights(values, label_names, g_tab, scale):
    first = label_names[0] * NT + label_names[2]
    second = label_names[1] * NT + label_names[2]
    g1r = g_tab[0][first]
    g1i = g_tab[1][first]
    g2r = g_tab[0][second]
    g2i = g_tab[1][second]
    real_gain = g1r * g2r + g1i * g2i
    imag_gain = g1i * g2r - g1r * g2i
    wreal = scale * (values[0] * real_gain - values[1] * imag_gain)
    wimag = scale * (values[0] * imag_gain + values[1] * real_gain)
    return (wreal, wimag)


def fold_columns(field):
    edges = jnp.concatenate([field[:, :M], field[:, -M:]], 1)
    extended = extended_2(edges, (("fcol", 1),), M)
    inner = field[:, M:-M]
    return jnp.concatenate(
        [inner[:, :M] + extended[:, :M], inner[:, M:-M], inner[:, -M:] + extended[:, -M:]], 1
    )


def fold_rows(field):
    edges = jnp.concatenate([field[:M], field[-M:]], 0)
    extended = extended_2(edges, (("frow", 0),), M)
    inner = field[M:-M]
    return jnp.concatenate([inner[:M] + extended[:M], inner[M:-M], inner[-M:] + extended[-M:]], 0)


def shards(
    vis,
    station_pairs,
    visibility_time_slot,
    station_u_cells,
    station_v_cells,
    facet_station_gains,
    holder_device_order,
):
    count_rows = lax.axis_size("frow")
    count_cols = lax.axis_size("fcol")
    n_rows = R * count_rows
    n_cols = C * count_cols
    frow_at = lax.axis_index("frow")
    fcol_at = lax.axis_index("fcol")
    g_tab = facet_station_gains[0, 0]
    label_names = jnp.concatenate([station_pairs, visibility_time_slot[None, :]], 0)
    block_size = vis.shape[1]
    scale = 0.5 / math.sqrt(NBLK * block_size)
    rows = frow_at * R - M + jnp.arange(R + 2 * M, dtype=jnp.int32)
    cols = fcol_at * C - M + jnp.arange(C + 2 * M, dtype=jnp.int32)
    total = jnp.zeros((R + 2 * M, C + 2 * M), jnp.float32)
    for step in range(NBLK):
        owner = holder_device_order[step]
        values, tag_names = (
            broadcast(vis, ("frow", "fcol"), owner),
            broadcast(label_names, ("frow", "fcol"), owner),
        )
        wreal, wimag = block_weights(values, tag_names, g_tab, scale)
        frequency_u = station_u_cells[tag_names[0]] - station_u_cells[tag_names[1]]
        frequency_v = station_v_cells[tag_names[0]] - station_v_cells[tag_names[1]]
        theta = phase_angles(frequency_u, rows, n_rows)
        phi = phase_angles(frequency_v, cols, n_cols).T
        row_table = jnp.concatenate([jnp.cos(theta), jnp.sin(theta)], 1).astype(jnp.bfloat16)
        top = wreal[:, None] * jnp.cos(phi) - wimag[:, None] * jnp.sin(phi)
        bottom = -(wimag[:, None] * jnp.cos(phi) + wreal[:, None] * jnp.sin(phi))
        col_table = jnp.concatenate([top, bottom], 0).astype(jnp.bfloat16)
        total = total + jnp.dot(row_table, col_table, preferred_element_type=jnp.float32)
    tapered = total * taper_line(R)[:, None] * taper_line(C)[None, :]
    image = fold_rows(fold_columns(tapered))
    return image


def solution(mesh):
    return jax.shard_map(
        shards,
        mesh=mesh,
        in_specs=(
            P(None, ("frow", "fcol")),
            P(None, ("frow", "fcol")),
            P(("frow", "fcol")),
            P(),
            P(),
            P("frow", "fcol", None, None),
            P(),
        ),
        out_specs=P("frow", "fcol"),
        check_vma=False,
    )
```

profile of v0, /device:TPU:71, one launch (start us, length us, event | category | flops | bytes accessed | tf_op | source)
XLA Modules:
  0.0 365.5 jit_solution(12329082438858966034)
XLA Ops:
  4.7 105.5 %all-reduce = (s32[3,256]{1,0:T(4,128)S(1)}, s32[3,256]{1,0:T(4,128)S(1)}, s32[3,256]{1,0:T(4,128)S(1)}, s32[3,256]{1,0:T(4,128)S(1)}) all-reduce(s32[3,256]{1,0:T(4,128)S(1)} %get-tuple-element.78, s32[3,256]{1,0:T(4,128)S(1)} %get-tuple-element.76, ...), channel_id=1, replica_groups=mesh['frow'=16,'fcol'=32] {'frow','fcol'}, use_global_device_ids=true, to_apply=%region_0.1 | all-reduce | flops 3072 | bytes 24576 | tf_op jit(solution)/shard_map/psum | solution.py:30
  121.7 1.7 gather_fusion.3
  123.4 1.7 gather_fusion.5
  125.2 1.7 gather_fusion.26
  139.1 1.9 gather_fusion.6
  141.1 1.9 gather_fusion.7
  143.0 1.9 gather_fusion
  145.0 1.9 gather_fusion.1
  147.0 1.9 gather_fusion.22
  148.9 1.9 gather_fusion.16
  150.9 1.9 gather_fusion.23
  152.8 1.9 gather_fusion.17
  154.8 1.9 gather_fusion.14
  156.8 1.9 gather_fusion.8
  158.7 1.9 gather_fusion.15
  160.7 1.9 gather_fusion.9
  162.6 1.9 gather_fusion.30
  164.6 1.9 gather_fusion.24
  166.6 1.9 gather_fusion.31
  168.5 1.9 gather_fusion.25
  170.6 99.6 %all-reduce.1 = (f32[2,256]{1,0:T(2,128)S(1)}, f32[2,256]{1,0:T(2,128)S(1)}, f32[2,256]{1,0:T(2,128)S(1)}, f32[2,256]{1,0:T(2,128)S(1)}) all-reduce(f32[2,256]{1,0:T(2,128)S(1)} %get-tuple-element.89, f32[2,256]{1,0:T(2,128)S(1)} %get-tuple-element.88, ...), channel_id=1, replica_groups=mesh['frow'=16,'fcol'=32] {'frow','fcol'}, use_global_device_ids=true, to_apply=%region_1.2 | all-reduce | flops 2048 | bytes 16384 | tf_op jit(solution)/shard_map/psum | solution.py:30
  270.5 19.1 %cosine_convert_fusion = (bf16[1152,256]{1,0:T(8,128)(2,1)S(1)}, bf16[1152,256]{1,0:T(8,128)(2,1)S(1)}, bf16[1152,256]{1,0:T(8,128)(2,1)S(1)}, bf16[1152,256]{1,...) fusion(s32[1152]{0:T(1024)S(1)} %add_select_fusion.8, ...), kind=kLoop, calls=%fused_computation.97 | loop fusion | flops 18874368 | bytes 4727296 | tf_op jit(solution)/shard_map/convert.2
  289.6 11.5 %subtract_convert_fusion = (bf16[256,640]{1,0:T(8,128)(2,1)S(1)}, bf16[256,640]{1,0:T(8,128)(2,1)S(1)}, bf16[256,640]{1,0:T(8,128)(2,1)S(1)}, bf16[256,640]{1,0:...) fusion(f32[256]{0:T(256)S(1)} %add_multiply_fusion, ...), kind=kLoop, calls=%fused_computation.137 | loop fusion | flops 15073280 | bytes 2636288 | tf_op jit(solution)/shard_map/convert
  305.5 6.8 %collective-permute-start = (f32[1152,64]{0,1:T(8,128)S(1)}, f32[1152,64]{0,1:T(8,128)S(1)}, u32[]{:S(2)}, u32[]{:S(2)}) collective-permute-start(f32[1152,64]{0,1:T(8,128)S(1)} %slice.281), channel_id=1, source_target_pairs={{0,1},{1,2},{2,3},{3,4},{4,5},{5,6},{6,7},{7,8},{8,9},{9,10},{10,1... | collective-permute-start | bytes 884744 | tf_op jit(solution)/shard_map/ppermute | solution.py:22
  312.3 10.0 %collective-permute-done = f32[1152,64]{0,1:T(8,128)S(1)} collective-permute-done((f32[1152,64]{0,1:T(8,128)S(1)}, f32[1152,64]{0,1:T(8,128)S(1)}, u32[]{:S(2)}, u32[]{:S(2)}) %collective-permute-start) | collective-permute-done | bytes 294944 | tf_op jit(solution)/shard_map/ppermute | solution.py:22
  322.4 1.9 collective-permute-start.1
  324.4 20.4 %collective-permute-done.1 = f32[1152,64]{0,1:T(8,128)S(1)} collective-permute-done((f32[1152,64]{0,1:T(8,128)S(1)}, f32[1152,64]{0,1:T(8,128)S(1)}, u32[]{:S(2)}, u32[]{:S(2)}) %collective-permute-start.1) | collective-permute-done | bytes 294944 | tf_op jit(solution)/shard_map/ppermute | solution.py:23
  345.1 1.9 collective-permute-start.2
  347.0 7.3 %collective-permute-done.2 = f32[64,512]{0,1:T(8,128)S(1)} collective-permute-done((f32[64,512]{0,1:T(8,128)S(1)}, f32[64,512]{0,1:T(8,128)S(1)}, u32[]{:S(2)}, u32[]{:S(2)}) %collective-permute-start.2) | collective-permute-done | bytes 131104 | tf_op jit(solution)/shard_map/ppermute | solution.py:22
  354.4 1.9 collective-permute-start.3
  358.0 3.6 collective-permute-done.3
  363.7 1.8 copy.9
  (80 shorter events, 34.6 us)
Async XLA Ops:
  0.0 139.1 %copy-start = (s32[512]{0:T(512)S(1)}, s32[512]{0:T(512)}, u32[]{:S(2)}) copy-start(s32[512]{0:T(512)} %param.11) | copy-start | bytes 6148
  139.1 4.0 %copy-start.1 = (s32[512]{0:T(512)S(1)}, s32[512]{0:T(512)}, u32[]{:S(2)}) copy-start(s32[512]{0:T(512)} %param.10) | copy-start | bytes 6148
  166.6 4.0 %copy-start.3 = (f32[2,256]{1,0:T(2,128)S(1)}, f32[2,256]{1,0:T(2,128)}, u32[]{:S(2)}) copy-start(f32[2,256]{1,0:T(2,128)} %param.7) | copy-start | bytes 6148
  305.5 16.8 %collective-permute-start = (f32[1152,64]{0,1:T(8,128)S(1)}, f32[1152,64]{0,1:T(8,128)S(1)}, u32[]{:S(2)}, u32[]{:S(2)}) collective-permute-start(f32[1152,64]{0,1:T(8,128)S(1)} %slice.281), channel_id=1, source_target_pairs={{0,1},{1,2},{2,3},{3,4},{4,5},{5,6},{6,7},{7,8},{8,9},{9,10},{10,1... | collective-permute-start | bytes 884744 | tf_op jit(solution)/shard_map/ppermute | solution.py:22
  322.4 22.5 %collective-permute-start.1 = (f32[1152,64]{0,1:T(8,128)S(1)}, f32[1152,64]{0,1:T(8,128)S(1)}, u32[]{:S(2)}, u32[]{:S(2)}) collective-permute-start(f32[1152,64]{0,1:T(8,128)S(1)} %get-tuple-element.26), channel_id=1, source_target_pairs={{1,0},{2,1},{3,2},{4,3},{5,4},{6,5},{7,6},{8,7},{9,8},{10,9},{11,1... | collective-permute-start | bytes 884744 | tf_op jit(solution)/shard_map/ppermute | solution.py:23
  345.1 9.2 %collective-permute-start.2 = (f32[64,512]{0,1:T(8,128)S(1)}, f32[64,512]{0,1:T(8,128)S(1)}, u32[]{:S(2)}, u32[]{:S(2)}) collective-permute-start(f32[64,512]{0,1:T(8,128)S(1)} %pad_maximum_fusion.3), channel_id=1, source_target_pairs={{0,32},{32,64},{64,96},{96,128},{128,160},{160,192},{192,224},{224... | collective-permute-start | bytes 393224 | tf_op jit(solution)/shard_map/ppermute | solution.py:22
  354.4 7.1 %collective-permute-start.3 = (f32[64,512]{0,1:T(8,128)S(1)}, f32[64,512]{0,1:T(8,128)S(1)}, u32[]{:S(2)}, u32[]{:S(2)}) collective-permute-start(f32[64,512]{0,1:T(8,128)S(1)} %get-tuple-element.28), channel_id=1, source_target_pairs={{32,0},{64,32},{96,64},{128,96},{160,128},{192,160},{224,192},{256... | collective-permute-start | bytes 393224 | tf_op jit(solution)/shard_map/ppermute | solution.py:23
  356.5 1.4 copy-start.2
  361.5 1.5 slice-start
where the time goes:
time: 366 us
  blocking collectives  205 us (56%)
  local copies, waits for them, and re-layouts  66 us (18%)
  waiting for transfers between devices  41.3 us (11%)
  other arithmetic  32.8 us (9%)
  starting transfers between devices  12.6 us (3%)
  matrix products  4.44 us (1%)
    psum x2, blocking collectives, broadcast(): return lax.psum(kept, axis)  205 us
    another operation x2, other arithmetic  30.5 us
    ppermute x2, waiting for transfers between devices, extended_2(): after = lax.ppermute(leading, axis, down)  24 us
    ppermute x2, waiting for transfers between devices, extended_2(): before = lax.ppermute(last, axis, up)  17.3 us
    gather x8, local copies, waits for them, and re-layouts, shards(): frequency_u = station_u_cells[tag_names[0]] - station_u_cells[tag_names[1]]  15.6 us
    gather x8, local copies, waits for them, and re-layouts, shards(): frequency_v = station_v_cells[tag_names[0]] - station_v_cells[tag_names[1]]  15.6 us
    ppermute x2, starting transfers between devices, extended_2(): before = lax.ppermute(last, axis, up)  8.72 us
  transfers between devices with their start and end apart: 4, of which 4 were waited for; matrix products, arithmetic and copies ran while one was open for 0% of the time, Pallas kernels for 0%

commit v1 on v0

v1 whole, which is shorter than its diff:
```python
import math

import jax
import jax.numpy as jnp
from jax import lax
from jax.experimental import pallas as pl
from jax.experimental.pallas import tpu as pltpu
from jax.sharding import PartitionSpec as P

R = 1024
C = 512
M = 64
NT = 16
NBLK = 4
BLOCK = 256
K = NBLK * BLOCK
N_FROW = 16
N_FCOL = 32
LANES = 128
SUB = 8
GROUPS = K // LANES
SIZE = R * N_FROW
PLANE = 32
DEPTH = 16
PIECES = 10
GAIN_ROWS = 64
MESH = pl.DeviceIdType.MESH
AROUND = [(dr, dc) for dr in (-1, 0, 1) for dc in (-1, 0, 1) if (dr, dc) != (0, 0)]


def place(dr, dc):
    return (1 + dr) * 3 + 1 + dc


def exchange_kernel(
    order_ref, vis_ref, pairs_ref, slot_ref, gains_ref, out_ref, around_ref,
    pay, raw, part, line, done, send1, recv1, send2, recv2, send3, recv3, send_g, recv_g,
):
    fr, fc = lax.axis_index("frow"), lax.axis_index("fcol")
    z_lo, y = fr // 4, fr % 4
    z_hi, xc = fc // 8, fc % 8
    me = y * 8 + xc
    my_z = z_hi * 4 + z_lo
    mine = me // 3
    reduces = jnp.logical_and(me % 3 == 0, mine < PIECES)

    def in_plane(s):
        return (z_lo * 4 + s // 8, z_hi * 8 + s % 8)

    def in_line(z):
        return ((z % 4) * 4 + y, (z // 4) * 8 + xc)

    def inside(dr, dc):
        row, col = fr + dr, fc + dc
        return (row >= 0) & (row < N_FROW) & (col >= 0) & (col < N_FCOL)

    barrier = pltpu.get_barrier_semaphore()

    def greet_plane(t, carry):
        pl.semaphore_signal(barrier, inc=1, device_id=in_plane((me + t) % PLANE), device_id_type=MESH)
        return carry

    lax.fori_loop(1, PLANE, greet_plane, 0)

    @pl.when(reduces)
    def _():
        def greet_line(t, carry):
            pl.semaphore_signal(barrier, inc=1, device_id=in_line((my_z + t) % DEPTH), device_id_type=MESH)
            return carry

        lax.fori_loop(1, DEPTH, greet_line, 0)

    count = PLANE - 1 + jnp.where(reduces, DEPTH - 1, 0)
    for dr, dc in AROUND:
        count = count + inside(dr, dc).astype(jnp.int32)

        @pl.when(inside(dr, dc))
        def _():
            pl.semaphore_signal(barrier, inc=1, device_id=(fr + dr, fc + dc), device_id_type=MESH)

    for half in range(2):
        cols = slice(half * LANES, (half + 1) * LANES)
        pay[half] = vis_ref[0:1, cols]
        pay[2 + half] = vis_ref[1:2, cols]
        pay[4 + half] = pairs_ref[0:1, cols].astype(jnp.float32)
        pay[6 + half] = pairs_ref[1:2, cols].astype(jnp.float32)
        pay[8 + half] = slot_ref[0:1, cols].astype(jnp.float32)

    pl.semaphore_wait(barrier, count)

    def piece_copy(j):
        return pltpu.make_async_remote_copy(
            src_ref=pay.at[j], dst_ref=raw.at[me], send_sem=send1.at[j], recv_sem=recv1.at[me],
            device_id=in_plane(3 * j), device_id_type=MESH,
        )

    def gain_copy(dr, dc):
        return pltpu.make_async_remote_copy(
            src_ref=gains_ref, dst_ref=around_ref.at[place(-dr, -dc)],
            send_sem=send_g.at[place(dr, dc)], recv_sem=recv_g.at[place(-dr, -dc)],
            device_id=(fr + dr, fc + dc), device_id_type=MESH,
        )

    for j in range(PIECES):
        @pl.when(me != 3 * j)
        def _():
            piece_copy(j).start()

    for dr, dc in AROUND:
        @pl.when(inside(dr, dc))
        def _():
            gain_copy(dr, dc).start()

    def line_copy(t):
        return pltpu.make_async_remote_copy(
            src_ref=part, dst_ref=line.at[my_z], send_sem=send2.at[t], recv_sem=recv2.at[my_z],
            device_id=in_line((my_z + t) % DEPTH), device_id_type=MESH,
        )

    def done_copy(t):
        return pltpu.make_async_remote_copy(
            src_ref=done.at[mine], dst_ref=done.at[mine], send_sem=send3.at[t], recv_sem=recv3.at[mine],
            device_id=in_plane((me + t) % PLANE), device_id_type=MESH,
        )

    @pl.when(reduces)
    def _():
        raw[me] = pay[mine]

        def arrived(t, carry):
            s = (me + t) % PLANE
            pltpu.make_async_copy(raw.at[s], raw.at[s], recv1.at[s]).wait()
            return carry

        lax.fori_loop(1, PLANE, arrived, 0)
        s = lax.broadcasted_iota(jnp.int32, (PLANE, 1, LANES), 0)
        holder = (z_lo * 4 + s // 8) * N_FCOL + z_hi * 8 + s % 8
        values = raw[...]
        for b in range(NBLK):
            part[b : b + 1, :] = jnp.sum(jnp.where(holder == order_ref[b], values, 0.0), axis=0)

        def start_line(t, carry):
            line_copy(t).start()
            return carry

        lax.fori_loop(1, DEPTH, start_line, 0)
        line[my_z] = part[...]

        def line_arrived(t, carry):
            z = (my_z + t) % DEPTH
            pltpu.make_async_copy(line.at[z], line.at[z], recv2.at[z]).wait()
            return carry

        lax.fori_loop(1, DEPTH, line_arrived, 0)
        done[mine] = jnp.sum(line[...], axis=0)

        def start_done(t, carry):
            done_copy(t).start()
            return carry

        lax.fori_loop(1, PLANE, start_done, 0)

    for j in range(PIECES):
        @pl.when(me != 3 * j)
        def _():
            pltpu.make_async_copy(done.at[j], done.at[j], recv3.at[j]).wait()

    out_ref[...] = done[...]

    for j in range(PIECES):
        @pl.when(me != 3 * j)
        def _():
            piece_copy(j).wait_send()

    @pl.when(reduces)
    def _():
        def sent_line(t, carry):
            line_copy(t).wait_send()
            return carry

        def sent_done(t, carry):
            done_copy(t).wait_send()
            return carry

        lax.fori_loop(1, DEPTH, sent_line, 0)
        lax.fori_loop(1, PLANE, sent_done, 0)

    for dr, dc in AROUND:
        @pl.when(inside(dr, dc))
        def _():
            gain_copy(dr, dc).wait_send()
            slot = around_ref.at[place(dr, dc)]
            pltpu.make_async_copy(slot, slot, recv_g.at[place(dr, dc)]).wait()


def exchange(order, vis, pairs, slot, gains):
    vmem = pl.BlockSpec(memory_space=pltpu.VMEM)
    anywhere = pl.BlockSpec(memory_space=pl.ANY)
    dma = pltpu.SemaphoreType.DMA
    return pl.pallas_call(
        exchange_kernel,
        out_shape=(
            jax.ShapeDtypeStruct((PIECES, NBLK, LANES), jnp.float32),
            jax.ShapeDtypeStruct((9, GAIN_ROWS, 2, LANES), jnp.float32),
        ),
        in_specs=[pl.BlockSpec(memory_space=pltpu.SMEM), vmem, vmem, vmem, anywhere],
        out_specs=(vmem, anywhere),
        scratch_shapes=[
            pltpu.VMEM((PIECES, 1, LANES), jnp.float32),
            pltpu.VMEM((PLANE, 1, LANES), jnp.float32),
            pltpu.VMEM((NBLK, LANES), jnp.float32),
            pltpu.VMEM((DEPTH, NBLK, LANES), jnp.float32),
            pltpu.VMEM((PIECES, NBLK, LANES), jnp.float32),
            dma((PIECES,)), dma((PLANE,)), dma((DEPTH,)), dma((DEPTH,)),
            dma((PLANE,)), dma((PIECES,)), dma((9,)), dma((9,)),
        ],
        compiler_params=pltpu.CompilerParams(collective_id=0, has_side_effects=True),
        name="exchange",
    )(order, vis, pairs, slot, gains)


def circle(m):
    m = m & (2 * SIZE - 1)
    quarter = (m + SIZE // 4) >> 13
    x = (m - (quarter << 13)).astype(jnp.float32) * (math.pi / SIZE)
    x2 = x * x
    s = x * (1.0 + x2 * (-1 / 6 + x2 * (1 / 120 + x2 * (-1 / 5040 + x2 * (1 / 362880)))))
    c = 1.0 + x2 * (-1 / 2 + x2 * (1 / 24 + x2 * (-1 / 720 + x2 * (1 / 40320))))
    odd = (quarter & 1) == 1
    cos = jnp.where(odd, s, c)
    sin = jnp.where(odd, c, s)
    cos = jnp.where(((quarter + 1) & 2) == 2, -cos, cos)
    sin = jnp.where((quarter & 2) == 2, -sin, sin)
    return cos, sin


def take_lanes(row, index):
    return jnp.take_along_axis(row, index, axis=1, mode="promise_in_bounds")


HALF = R // 2
LOW = 32
HIGH = C // LOW
WIDE = 256
SETS = ((3, 4, 5), (0, 1, 2), (6, 7, 8))


def image_kernel(
    fin_ref, ucell_ref, vcell_ref, own_ref, around_ref, out_ref,
    w_scr, uv_scr, wave_u, wave_v, front, rows_c, rows_s, cols_a, cols_b,
):
    fr, fc = lax.axis_index("frow"), lax.axis_index("fcol")
    f32, i32 = jnp.float32, jnp.int32
    s1 = fin_ref[2].astype(i32)
    s2 = fin_ref[3].astype(i32)
    t = fin_ref[4].astype(i32)

    def station(ref):
        total = jnp.zeros((SUB, LANES), i32)
        for row in range(4):
            cells = jnp.broadcast_to(ref[row : row + 1, :], (SUB, LANES))
            one = take_lanes(cells, s1 & 127)
            two = take_lanes(cells, s2 & 127)
            total = total + jnp.where((s1 >> 7) == row, one, 0) - jnp.where((s2 >> 7) == row, two, 0)
        return total

    uv_scr[0] = station(ucell_ref)
    uv_scr[1] = station(vcell_ref)

    first, second = s1 * NT + t, s2 * NT + t
    lo1, hi1 = first & 127, first >> 7
    lo2, hi2 = second & 127, second >> 7

    def gather_row(row, carry):
        here1, here2 = hi1 == row, hi2 == row
        found = []
        for f in range(9):
            for part in range(2):
                where = 2 * row + part
                line = own_ref[pl.ds(where, 1), :] if f == 4 else around_ref[f, pl.ds(where, 1), :]
                line = jnp.broadcast_to(line, (SUB, LANES))
                a, b = carry[2 * len(found)], carry[2 * len(found) + 1]
                found.append((jnp.where(here1, take_lanes(line, lo1), a), jnp.where(here2, take_lanes(line, lo2), b)))
        return tuple(x for pair in found for x in pair)

    zero = jnp.zeros((SUB, LANES), f32)
    gains = lax.fori_loop(0, GAIN_ROWS, gather_row, (zero,) * 36)
    scale = 0.5 / math.sqrt(K)
    v_r, v_i = fin_ref[0], fin_ref[1]
    for f in range(9):
        g1r, g2r, g1i, g2i = gains[4 * f : 4 * f + 4]
        real_gain = g1r * g2r + g1i * g2i
        imag_gain = g1i * g2r - g1r * g2i
        w_r = scale * (v_r * real_gain - v_i * imag_gain)
        w_i = scale * (v_r * imag_gain + v_i * real_gain)
        row, col = fr + f // 3 - 1, fc + f % 3 - 1
        inside = (row >= 0) & (row < N_FROW) & (col >= 0) & (col < N_FCOL)
        w_scr[2 * f] = jnp.where(inside, w_r, 0.0)
        w_scr[2 * f + 1] = jnp.where(inside, w_i, 0.0)

    centre = fr * (2 * R) + R - 1
    low = lax.broadcasted_iota(i32, (LOW, LANES), 0)
    high = lax.broadcasted_iota(i32, (HIGH, LANES), 0)

    def tables(g, carry):
        lanes = pl.ds(pl.multiple_of(g * LANES, LANES), LANES)
        u = uv_scr[0, pl.ds(g, 1), :]
        v = uv_scr[1, pl.ds(g, 1), :]
        lc, ls = circle(u * (2 * low + 1))
        hc, hs = circle(u * (2 * LOW * high))
        wave_u[0] = hc
        wave_u[1] = hs
        for h in range(HIGH):
            bc, bs = wave_u[0, h : h + 1, :], wave_u[1, h : h + 1, :]
            rows_c[h * LOW : (h + 1) * LOW, lanes] = (bc * lc - bs * ls).astype(jnp.bfloat16)
            rows_s[h * LOW : (h + 1) * LOW, lanes] = (bc * ls + bs * lc).astype(jnp.bfloat16)
        lc, ls = circle(v * (2 * low))
        wave_v[0, g] = lc
        wave_v[1, g] = ls
        pc, ps = circle(u * centre + v * (2 * (fc * C + LOW * high)))
        for f in range(9):
            w_r, w_i = w_scr[2 * f, pl.ds(g, 1), :], w_scr[2 * f + 1, pl.ds(g, 1), :]
            front[2 * f, g] = w_r * pc - w_i * ps
            front[2 * f + 1, g] = w_r * ps + w_i * pc
        return carry

    lax.fori_loop(0, GROUPS, tables, 0)

    lowf = low.astype(f32)

    def columns(chunk):
        def group(g, carry):
            lanes = pl.ds(pl.multiple_of(g * LANES, LANES), LANES)
            lc, ls = wave_v[0, g], wave_v[1, g]
            for n, (left, mid, right) in enumerate(SETS):
                for i in range(WIDE // LOW):
                    h = chunk * (WIDE // LOW) + i
                    w_r, w_i = front[2 * mid, g, h : h + 1, :], front[2 * mid + 1, g, h : h + 1, :]
                    if h * LOW < M or h * LOW >= C - M:
                        if h * LOW < M:
                            side = left
                            t_mid = (lowf + (h * LOW + M + 0.5)) * (1 / (2 * M))
                            t_side = (M - 0.5 - h * LOW - lowf) * (1 / (2 * M))
                        else:
                            side = right
                            t_mid = (C + M - 0.5 - h * LOW - lowf) * (1 / (2 * M))
                            t_side = (lowf + (h * LOW - C + M + 0.5)) * (1 / (2 * M))
                        w_r = t_mid * w_r + t_side * front[2 * side, g, h : h + 1, :]
                        w_i = t_mid * w_i + t_side * front[2 * side + 1, g, h : h + 1, :]
                    at = slice(i * LOW, (i + 1) * LOW)
                    cols_a[n, at, lanes] = (w_r * lc - w_i * ls).astype(jnp.bfloat16)
                    cols_b[n, at, lanes] = (w_r * ls + w_i * lc).astype(jnp.bfloat16)
            return carry

        lax.fori_loop(0, GROUPS, group, 0)

    def times(rows, cols):
        return lax.dot_general(rows, cols, (((1,), (1,)), ((), ())), preferred_element_type=f32)

    edge = HALF - M
    d = lax.broadcasted_iota(i32, (M, 1), 0).astype(f32)
    t_own = (2 * M - 0.5 - M - d + M) * (1 / (2 * M))
    t_next = (d + 0.5) * (1 / (2 * M))
    turn = SUB - 1 - lax.broadcasted_iota(i32, (SUB, LANES), 0)

    for chunk in range(C // WIDE):
        columns(chunk)
        at = slice(chunk * WIDE, (chunk + 1) * WIDE)
        even = times(rows_c[...], cols_a[0])
        odd = times(rows_s[...], cols_b[0])
        edge_c, edge_s = rows_c[edge:, :], rows_s[edge:, :]
        above = times(edge_c, cols_a[1]) + times(edge_s, cols_b[1])
        below = times(edge_c, cols_a[2]) - times(edge_s, cols_b[2])
        down = even - odd
        up = even + odd
        out_ref[HALF : R - M, at] = down[:edge]
        out_ref[R - M :, at] = down[edge:] * t_own + below * t_next
        up = jnp.concatenate([up[:edge], up[edge:] * t_own + above * t_next], 0)
        for i in range(HALF // SUB):
            for k in range(WIDE // LANES):
                tile = up[i * SUB : (i + 1) * SUB, k * LANES : (k + 1) * LANES]
                tile = jnp.take_along_axis(tile, turn, axis=0, mode="promise_in_bounds")
                out_ref[HALF - (i + 1) * SUB : HALF - i * SUB, chunk * WIDE + k * LANES : chunk * WIDE + (k + 1) * LANES] = tile


def image_of(fin, ucell, vcell, own, around):
    vmem = pl.BlockSpec(memory_space=pltpu.VMEM)
    return pl.pallas_call(
        image_kernel,
        out_shape=jax.ShapeDtypeStruct((R, C), jnp.float32),
        in_specs=[vmem] * 5,
        out_specs=vmem,
        scratch_shapes=[
            pltpu.VMEM((18, SUB, LANES), jnp.float32),
            pltpu.VMEM((2, SUB, LANES), jnp.int32),
            pltpu.VMEM((2, HIGH, LANES), jnp.float32),
            pltpu.VMEM((2, GROUPS, LOW, LANES), jnp.float32),
            pltpu.VMEM((18, GROUPS, HIGH, LANES), jnp.float32),
            pltpu.VMEM((HALF, K), jnp.bfloat16),
            pltpu.VMEM((HALF, K), jnp.bfloat16),
            pltpu.VMEM((3, WIDE, K), jnp.bfloat16),
            pltpu.VMEM((3, WIDE, K), jnp.bfloat16),
        ],
        compiler_params=pltpu.CompilerParams(vmem_limit_bytes=48 * 1024 * 1024),
        name="image",
    )(fin, ucell, vcell, own, around)


def shards(vis, station_pairs, visibility_time_slot, station_u_cells, station_v_cells, facet_station_gains, holder_device_order):
    gains = facet_station_gains.reshape(2, GAIN_ROWS, LANES).transpose(1, 0, 2)
    fin, around = exchange(holder_device_order, vis, station_pairs, visibility_time_slot.reshape(1, BLOCK), gains)
    return image_of(
        fin.reshape(5, 2 * NBLK, LANES),
        station_u_cells.reshape(4, LANES),
        station_v_cells.reshape(4, LANES),
        gains.reshape(2 * GAIN_ROWS, LANES),
        around.reshape(9, 2 * GAIN_ROWS, LANES),
    )


def solution(mesh):
    return jax.shard_map(
        shards,
        mesh=mesh,
        in_specs=(
            P(None, ("frow", "fcol")),
            P(None, ("frow", "fcol")),
            P(("frow", "fcol")),
            P(),
            P(),
            P("frow", "fcol", None, None),
            P(),
        ),
        out_specs=P("frow", "fcol"),
        check_vma=False,
    )
```

time: 366 us -> 58.1 us (0.16)
  the two profiles are of different devices: /device:TPU:71 before, /device:TPU:59 now
where the time goes in v1:
time: 58.1 us; the launch traced here: 57.7 us
  Pallas kernels  53.7 us (92%)
  local copies, waits for them, and re-layouts  3.99 us (7%)
    pallas_call x1, Pallas kernels, exchange(): pl.pallas_call(exchange_kernel, out_shape=(jax.ShapeDtypeStruct((PIECES,...  38.8 us
    pallas_call x1, Pallas kernels, image_of(): pl.pallas_call(image_kernel, out_shape=jax.ShapeDtypeStruct((R, C), jnp.f...  14.9 us
    unnamed x10, local copies, waits for them, and re-layouts  3.99 us

profile of v1, /device:TPU:59, one launch (start us, length us, event | category | flops | bytes accessed | tf_op | source)
XLA Modules:
  0.0 57.7 jit_solution(1330028796901617331)
XLA Ops:
  0.0 38.8 %exchange.1 = (f32[10,4,128]{2,1,0:T(4,128)}, f32[9,64,2,128]{3,2,1,0:T(2,128)}) custom-call(s32[512]{0:T(512)} %order_ref.1, f32[2,256]{1,0:T(2,128)} %vis_ref.1, s32[2,256]{1,0:T(2,128)} %pairs_ref.1, s32[1,256]{1,0:T(1,128)} %bitcast.16, f32[64,2,128]{2,1,0:T(2,128)} %bitcast.11), custom_call_target="tpu_custom_call" | custom-call | tf_op jit(solution)/shard_map/exchange/pallas_call | solution.py:200
  38.8 0.0 copy-start
  38.8 1.1 %copy-done = f32[9,64,2,128]{3,2,1,0:T(2,128)S(1)} copy-done((f32[9,64,2,128]{3,2,1,0:T(2,128)S(1)}, f32[9,64,2,128]{3,2,1,0:T(2,128)}, u32[]{:S(2)}) %copy-start) | copy-done | bytes 589848
  39.9 0.0 copy-start.1
  39.9 0.8 %copy-done.1 = f32[1,1,2,8192]{3,2,1,0:T(2,128)S(1)} copy-done((f32[1,1,2,8192]{3,2,1,0:T(2,128)S(1)}, f32[1,1,2,8192]{3,2,1,0:T(2,128)}, u32[]{:S(2)}) %copy-start.1) | copy-done | bytes 65560
  40.7 0.0 copy-start.2
  40.7 0.7 %copy-done.2 = f32[10,4,128]{2,1,0:T(4,128)S(1)} copy-done((f32[10,4,128]{2,1,0:T(4,128)S(1)}, f32[10,4,128]{2,1,0:T(4,128)}, u32[]{:S(2)}) %copy-start.2) | copy-done | bytes 20504
  41.5 0.0 copy-start.3
  41.5 0.7 %copy-done.3 = s32[512]{0:T(512)S(1)} copy-done((s32[512]{0:T(512)S(1)}, s32[512]{0:T(512)}, u32[]{:S(2)}) %copy-start.3) | copy-done | bytes 2072
  42.2 0.0 copy-start.4
  42.2 0.7 %copy-done.4 = s32[512]{0:T(512)S(1)} copy-done((s32[512]{0:T(512)S(1)}, s32[512]{0:T(512)}, u32[]{:S(2)}) %copy-start.4) | copy-done | bytes 2072
  42.8 14.9 %image.1 = f32[1024,512]{1,0:T(8,128)} custom-call(f32[5,8,128]{2,1,0:T(8,128)S(1)} %bitcast.13, s32[4,128]{1,0:T(4,128)S(1)} %bitcast.14, s32[4,128]{1,0:T(4,128)S(1)} %bitcast.15, f32[128,128]{1,0:T(8,128)S(1)} %bitcast.12, f32[9,128,128]{2,1,0:T(8,128)S(1)} %bitcast.10), custom_call_target="tpu_custom_call" | custom-call | tf_op jit(solution)/shard_map/image/pallas_call | solution.py:388
Async XLA Ops:
  38.8 1.1 %copy-start = (f32[9,64,2,128]{3,2,1,0:T(2,128)S(1)}, f32[9,64,2,128]{3,2,1,0:T(2,128)}, u32[]{:S(2)}) copy-start(f32[9,64,2,128]{3,2,1,0:T(2,128)} %get-tuple-element.8) | copy-start | bytes 1769476
  39.9 0.8 %copy-start.1 = (f32[1,1,2,8192]{3,2,1,0:T(2,128)S(1)}, f32[1,1,2,8192]{3,2,1,0:T(2,128)}, u32[]{:S(2)}) copy-start(f32[1,1,2,8192]{3,2,1,0:T(2,128)} %param.12) | copy-start | bytes 196612
  40.7 0.7 %copy-start.2 = (f32[10,4,128]{2,1,0:T(4,128)S(1)}, f32[10,4,128]{2,1,0:T(4,128)}, u32[]{:S(2)}) copy-start(f32[10,4,128]{2,1,0:T(4,128)} %get-tuple-element.7) | copy-start | bytes 61444
  41.5 0.7 %copy-start.3 = (s32[512]{0:T(512)S(1)}, s32[512]{0:T(512)}, u32[]{:S(2)}) copy-start(s32[512]{0:T(512)} %param.10) | copy-start | bytes 6148
  42.2 0.7 %copy-start.4 = (s32[512]{0:T(512)S(1)}, s32[512]{0:T(512)}, u32[]{:S(2)}) copy-start(s32[512]{0:T(512)} %param.11) | copy-start | bytes 6148

commit v2 on v0

v2 whole, which is shorter than its diff:
```python
import math

import jax
import jax.numpy as jnp
from jax import lax
from jax.experimental import pallas as pl
from jax.experimental.pallas import tpu as pltpu
from jax.sharding import PartitionSpec as P

R = 1024
C = 512
M = 64
NT = 16
NBLK = 4
BLOCK = 256
K = NBLK * BLOCK
N_FROW = 16
N_FCOL = 32
LANES = 128
SUB = 8
GROUPS = K // LANES
SIZE = R * N_FROW
PLANE = 32
DEPTH = 16
PIECES = 10
GAIN_ROWS = 64
MESH = pl.DeviceIdType.MESH
AROUND = [(dr, dc) for dr in (-1, 0, 1) for dc in (-1, 0, 1) if (dr, dc) != (0, 0)]


def place(dr, dc):
    return (1 + dr) * 3 + 1 + dc


def circle(m):
    m = m & (2 * SIZE - 1)
    quarter = (m + SIZE // 4) >> 13
    x = (m - (quarter << 13)).astype(jnp.float32) * (math.pi / SIZE)
    x2 = x * x
    s = x * (1.0 + x2 * (-1 / 6 + x2 * (1 / 120 + x2 * (-1 / 5040 + x2 * (1 / 362880)))))
    c = 1.0 + x2 * (-1 / 2 + x2 * (1 / 24 + x2 * (-1 / 720 + x2 * (1 / 40320))))
    odd = (quarter & 1) == 1
    cos = jnp.where(odd, s, c)
    sin = jnp.where(odd, c, s)
    cos = jnp.where(((quarter + 1) & 2) == 2, -cos, cos)
    sin = jnp.where((quarter & 2) == 2, -sin, sin)
    return cos, sin


def take_lanes(row, index):
    return jnp.take_along_axis(row, index, axis=1, mode="promise_in_bounds")


def exchange_kernel(
    order_hbm, vis_hbm, pairs_hbm, slot_hbm, ucell_hbm, vcell_hbm, gain_hbm, uv_ref, w_ref,
    order, vis, pairs, slot, ucell, vcell, gain, pay, raw, part, line, done, w_own, w_all,
    in_sem, send1, recv1, send2, recv2, send3, recv3, send_w, recv_w,
):
    fr, fc = lax.axis_index("frow"), lax.axis_index("fcol")
    f32, i32 = jnp.float32, jnp.int32
    z_lo, y = lax.div(fr, 4), lax.rem(fr, 4)
    z_hi, xc = lax.div(fc, 8), lax.rem(fc, 8)
    me = y * 8 + xc
    my_z = z_hi * 4 + z_lo
    mine = lax.div(me, 3)
    reduces = jnp.logical_and(lax.rem(me, 3) == 0, mine < PIECES)
    plane_row, plane_col = z_lo * 4, z_hi * 8

    def in_plane(s):
        return (plane_row + s // 8, plane_col + s % 8)

    def in_line(z):
        return ((z % 4) * 4 + y, (z // 4) * 8 + xc)

    def inside(dr, dc):
        row, col = fr + dr, fc + dc
        return (row >= 0) & (row < N_FROW) & (col >= 0) & (col < N_FCOL)

    barrier = pltpu.get_barrier_semaphore()

    def greet(device):
        pl.semaphore_signal(barrier, inc=1, device_id=device, device_id_type=MESH)

    @pl.when(reduces)
    def _():
        for z in range(DEPTH):
            @pl.when(my_z != z)
            def _():
                greet(in_line(z))

        for s in range(PLANE):
            @pl.when(me != s)
            def _():
                greet(in_plane(s))

    @pl.when(jnp.logical_not(reduces))
    def _():
        for j in range(PIECES):
            greet(in_plane(3 * j))

    count = jnp.where(reduces, PLANE - 1 + DEPTH - 1, PIECES)
    for dr, dc in AROUND:
        count = count + inside(dr, dc).astype(i32)

        @pl.when(inside(dr, dc))
        def _():
            greet((fr + dr, fc + dc))

    loads = ((vis_hbm, vis), (pairs_hbm, pairs), (slot_hbm, slot), (order_hbm, order), (ucell_hbm, ucell), (vcell_hbm, vcell), (gain_hbm, gain))
    loads = [pltpu.make_async_copy(a, b, in_sem.at[n]) for n, (a, b) in enumerate(loads)]
    for load in loads:
        load.start()
    for dr, dc in AROUND:
        @pl.when(jnp.logical_not(inside(dr, dc)))
        def _():
            w_all[place(dr, dc)] = jnp.zeros((2, SUB, LANES), f32)

    for load in loads:
        load.wait()
    for half in range(2):
        cols = slice(half * LANES, (half + 1) * LANES)
        pay[half] = vis[0:1, cols]
        pay[2 + half] = vis[1:2, cols]
        pay[4 + half] = pairs[0:1, cols].astype(f32)
        pay[6 + half] = pairs[1:2, cols].astype(f32)
        pay[8 + half] = slot[0:1, cols].astype(f32)

    pl.semaphore_wait(barrier, count)

    def piece_copy(j):
        return pltpu.make_async_remote_copy(
            src_ref=pay.at[j], dst_ref=raw.at[me], send_sem=send1.at[j], recv_sem=recv1,
            device_id=in_plane(3 * j), device_id_type=MESH,
        )

    def line_copy(z):
        return pltpu.make_async_remote_copy(
            src_ref=part, dst_ref=line.at[my_z], send_sem=send2.at[z], recv_sem=recv2,
            device_id=in_line(z), device_id_type=MESH,
        )

    def done_copy(s):
        return pltpu.make_async_remote_copy(
            src_ref=done.at[mine], dst_ref=done.at[mine], send_sem=send3.at[s], recv_sem=recv3,
            device_id=in_plane(s), device_id_type=MESH,
        )

    def weight_copy(dr, dc):
        return pltpu.make_async_remote_copy(
            src_ref=w_own, dst_ref=w_all.at[place(-dr, -dc)],
            send_sem=send_w.at[place(dr, dc)], recv_sem=recv_w.at[place(-dr, -dc)],
            device_id=(fr + dr, fc + dc), device_id_type=MESH,
        )

    def landed(ref, slots, sem):
        view = ref.at[pl.ds(0, slots)]
        pltpu.make_async_copy(view, view, sem).wait()

    for j in range(PIECES):
        @pl.when(me != 3 * j)
        def _():
            piece_copy(j).start()

    @pl.when(reduces)
    def _():
        raw[me] = pay[mine]
        s = lax.broadcasted_iota(i32, (PLANE, 1, LANES), 0)
        holder = (plane_row + (s >> 3)) * N_FCOL + plane_col + (s & 7)
        landed(raw, PLANE - 1, recv1)
        values = raw[...]
        for b in range(NBLK):
            part[b : b + 1, :] = jnp.sum(jnp.where(holder == order[b], values, 0.0), axis=0)
        for z in range(DEPTH):
            @pl.when(my_z != z)
            def _():
                line_copy(z).start()

        line[my_z] = part[...]
        landed(line, DEPTH - 1, recv2)
        done[mine] = jnp.sum(line[...], axis=0)
        for s in range(PLANE):
            @pl.when(me != s)
            def _():
                done_copy(s).start()

        landed(done, PIECES - 1, recv3)

    @pl.when(jnp.logical_not(reduces))
    def _():
        landed(done, PIECES, recv3)

    def value(v):
        return jnp.concatenate([done[2 * v], done[2 * v + 1]], 0)

    s1, s2, t = value(2).astype(i32), value(3).astype(i32), value(4).astype(i32)
    first, second = s1 * NT + t, s2 * NT + t

    def pick(part, index):
        lane, row = index & 127, index >> 7
        bits = [(row & (1 << b)) != 0 for b in range(6)]
        stack = []
        for n in range(GAIN_ROWS):
            values = jnp.broadcast_to(gain[2 * n + part : 2 * n + part + 1, :], (SUB, LANES))
            found, level = take_lanes(values, lane), 0
            while stack and stack[-1][0] == level:
                found = jnp.where(bits[level], found, stack.pop()[1])
                level += 1
            stack.append((level, found))
        return stack[0][1]

    scale = 0.5 / math.sqrt(K)
    v_r, v_i = value(0), value(1)
    g1r, g1i = pick(0, first), pick(1, first)
    g2r, g2i = pick(0, second), pick(1, second)
    real_gain = g1r * g2r + g1i * g2i
    imag_gain = g1i * g2r - g1r * g2i
    w_own[0] = scale * (v_r * real_gain - v_i * imag_gain)
    w_own[1] = scale * (v_r * imag_gain + v_i * real_gain)
    for dr, dc in AROUND:
        @pl.when(inside(dr, dc))
        def _():
            weight_copy(dr, dc).start()

    def station(ref):
        total = jnp.zeros((SUB, LANES), i32)
        for row in range(4):
            cells = jnp.broadcast_to(ref[row : row + 1, :], (SUB, LANES))
            one = take_lanes(cells, s1 & 127)
            two = take_lanes(cells, s2 & 127)
            total = total + jnp.where((s1 >> 7) == row, one, 0) - jnp.where((s2 >> 7) == row, two, 0)
        return total

    u, v = station(ucell), station(vcell)
    uv_ref[0] = u
    uv_ref[1] = v
    mid_c, mid_s = circle(u * (fr * (2 * R) + R - 1) + v * (2 * (fc * C + C // 2)))

    def turn(place_of, w_r, w_i):
        w_ref[2 * place_of] = w_r * mid_c - w_i * mid_s
        w_ref[2 * place_of + 1] = w_r * mid_s + w_i * mid_c

    turn(4, w_own[0], w_own[1])

    for j in range(PIECES):
        @pl.when(me != 3 * j)
        def _():
            piece_copy(j).wait_send()

    @pl.when(reduces)
    def _():
        for z in range(DEPTH):
            @pl.when(my_z != z)
            def _():
                line_copy(z).wait_send()

        for s in range(PLANE):
            @pl.when(me != s)
            def _():
                done_copy(s).wait_send()

    for dr, dc in AROUND:
        @pl.when(inside(dr, dc))
        def _():
            weight_copy(dr, dc).wait_send()
            slot_of = w_all.at[place(dr, dc)]
            pltpu.make_async_copy(slot_of, slot_of, recv_w.at[place(dr, dc)]).wait()

    for dr, dc in AROUND:
        turn(place(dr, dc), w_all[place(dr, dc), 0], w_all[place(dr, dc), 1])


def exchange(order, vis, pairs, slot, ucell, vcell, gain):
    vmem = pl.BlockSpec(memory_space=pltpu.VMEM)
    dma = pltpu.SemaphoreType.DMA
    f32, i32 = jnp.float32, jnp.int32
    return pl.pallas_call(
        exchange_kernel,
        out_shape=(jax.ShapeDtypeStruct((2, SUB, LANES), i32), jax.ShapeDtypeStruct((18, SUB, LANES), f32)),
        in_specs=[pl.BlockSpec(memory_space=pl.ANY)] * 7,
        out_specs=(vmem, vmem),
        scratch_shapes=[
            pltpu.SMEM((N_FROW * N_FCOL,), i32),
            pltpu.VMEM((2, BLOCK), f32),
            pltpu.VMEM((2, BLOCK), i32),
            pltpu.VMEM((1, BLOCK), i32),
            pltpu.VMEM((4, LANES), i32),
            pltpu.VMEM((4, LANES), i32),
            pltpu.VMEM((2 * GAIN_ROWS, LANES), f32),
            pltpu.VMEM((PIECES, 1, LANES), f32),
            pltpu.VMEM((PLANE, 1, LANES), f32),
            pltpu.VMEM((NBLK, LANES), f32),
            pltpu.VMEM((DEPTH, NBLK, LANES), f32),
            pltpu.VMEM((PIECES, NBLK, LANES), f32),
            pltpu.VMEM((2, SUB, LANES), f32),
            pltpu.VMEM((9, 2, SUB, LANES), f32),
            dma((7,)), dma((PIECES,)), dma, dma((DEPTH,)), dma, dma((PLANE,)), dma, dma((9,)), dma((9,)),
        ],
        compiler_params=pltpu.CompilerParams(collective_id=0, has_side_effects=True),
        name="exchange",
    )(order, vis, pairs, slot, ucell, vcell, gain)


HALF = R // 2
LOW = 32
WIDE = 256
EDGE = HALF - M
INNER = tuple(range(-4, 4))
OUTER = tuple(range(-8, -4)) + tuple(range(4, 8))


def image_kernel(
    uv_hbm, w_hbm, out_hbm,
    uv_scr, w_scr, turn_u, turn_v, wave_v, rows_c, rows_s,
    cols_a, cols_b, plain_c, plain_s, edge_r, edge_i, image, in_sem, out_sem,
):
    f32, i32, bf16 = jnp.float32, jnp.int32, jnp.bfloat16
    loads = [pltpu.make_async_copy(uv_hbm, uv_scr, in_sem.at[0]), pltpu.make_async_copy(w_hbm, w_scr, in_sem.at[1])]
    for load in loads:
        load.start()
    for load in loads:
        load.wait()
    low = lax.broadcasted_iota(i32, (LOW, LANES), 0)
    step = lax.broadcasted_iota(i32, (SUB, LANES), 0) + 1

    def row_tables(g):
        u = uv_scr[0, pl.ds(g, 1), :]
        v = uv_scr[1, pl.ds(g, 1), :]
        lc, ls = circle(u * (2 * low + 1 + HALF))
        hc, hs = circle(u * (2 * LOW * step))
        turn_u[0] = hc
        turn_u[1] = hs

        def put(block, c, s):
            at = slice((block + 8) * LOW, (block + 9) * LOW)
            rows_c[g, at, :] = c.astype(bf16)
            rows_s[g, at, :] = s.astype(bf16)

        put(0, lc, ls)
        for h in range(1, 9):
            bc, bs = turn_u[0, h - 1 : h, :], turn_u[1, h - 1 : h, :]
            cc, ss, cs, sc = lc * bc, ls * bs, lc * bs, ls * bc
            put(-h, cc + ss, sc - cs)
            if h < 8:
                put(h, cc - ss, sc + cs)
        lc, ls = circle(v * (2 * low))
        wave_v[0, g] = lc
        wave_v[1, g] = ls
        hc, hs = circle(v * (2 * LOW * step))
        turn_v[0, g] = hc
        turn_v[1, g] = hs

    def prepare(n, carry):
        row_tables(n)
        return carry

    lax.fori_loop(0, GROUPS, prepare, 0)

    lowf = low.astype(f32)

    def turned(g, h, real, imag):
        bc, bs = turn_v[0, g, h - 1 : h, :], turn_v[1, g, h - 1 : h, :]
        rc, ix, rs, ic = real * bc, imag * bs, real * bs, imag * bc
        return {h: (rc - ix, ic + rs), -h: (rc + ix, ic - rs)}

    def weighted(g, f, lc, ls):
        w_r, w_i = w_scr[2 * f, pl.ds(g, 1), :], w_scr[2 * f + 1, pl.ds(g, 1), :]
        return w_r * lc - w_i * ls, w_r * ls + w_i * lc

    def columns(g, blocks):
        lc, ls = wave_v[0, g], wave_v[1, g]
        z_r, z_i = weighted(g, 4, lc, ls)
        plain = {0: (lc, ls)}
        own = {0: (z_r, z_i)}
        for h in sorted({abs(b) for b in blocks} - {0}):
            plain.update(turned(g, h, lc, ls))
            own.update(turned(g, h, z_r, z_i))
        for f, side in ((3, [b for b in blocks if b < -6]), (5, [b for b in blocks if b > 5])):
            if side:
                s_r, s_i = weighted(g, f, lc, ls)
                d_r, d_i = z_r - s_r, z_i - s_i
            for b in side:
                start = (b + 8) * LOW
                if b < 0:
                    taper = (lowf + (start + M + 0.5)) * (1 / (2 * M))
                else:
                    taper = (C + M - 0.5 - start - lowf) * (1 / (2 * M))
                own[b] = turned(g, abs(b), s_r + taper * d_r, s_i + taper * d_i)[b]
        for n, b in enumerate(blocks):
            at = slice(n * LOW, (n + 1) * LOW)
            for refs, values in (((cols_a, cols_b), own[b]), ((plain_c, plain_s), plain[b])):
                refs[0][g, at, :] = values[0].astype(bf16)
                refs[1][g, at, :] = values[1].astype(bf16)

    def edges(g, side):
        u = uv_scr[0, pl.ds(g, 1), :]
        for half in range(M // LOW):
            c, s = edge_wave(g, u, half)
            for f, sign, at in ((side, -1.0, half * LOW), (6 + side, 1.0, M + half * LOW)):
                w_r, w_i = w_scr[2 * f, pl.ds(g, 1), :], w_scr[2 * f + 1, pl.ds(g, 1), :]
                if sign > 0:
                    real, minus = w_r * c - w_i * s, w_r * s + w_i * c
                else:
                    real, minus = w_r * c + w_i * s, w_i * c - w_r * s
                edge_r[side, g, at : at + LOW, :] = real.astype(bf16)
                edge_i[side, g, at : at + LOW, :] = (-minus).astype(bf16)

    def edge_wave(g, u, half):
        return circle(u * (2 * low + 1 + 2 * (EDGE + half * LOW)))

    def inner(g, carry):
        columns(g, INNER)
        edges(g, 1)
        return carry

    lax.fori_loop(0, GROUPS, inner, 0)

    def whole(ref, at=None):
        return jnp.concatenate([ref[g] if at is None else ref[at, g] for g in range(GROUPS)], 1)

    def times(rows, cols):
        return lax.dot_general(rows, cols, (((1,), (1,)), ((), ())), preferred_element_type=f32)

    d = lax.broadcasted_iota(i32, (M, 1), 0).astype(f32)
    t_own = (2 * M - 0.5 - d) * (1 / (2 * M))
    t_next = (d + 0.5) * (1 / (2 * M))
    flip = SUB - 1 - lax.broadcasted_iota(i32, (SUB, LANES), 0)

    def stitch(even, odd, above, below, starts):
        down = even - odd
        up = even + odd
        low_edge = down[EDGE:] * t_own + below * t_next
        high_edge = up[EDGE:] * t_own + above * t_next
        for k, start in enumerate(starts):
            at = slice(k * LANES, (k + 1) * LANES)
            to = slice(start, start + LANES)
            image[HALF : R - M, to] = down[:EDGE, at]
            image[R - M :, to] = low_edge[:, at]
            for i in range(HALF // SUB):
                tile = up[i * SUB : (i + 1) * SUB, at] if i < EDGE // SUB else high_edge[i * SUB - EDGE : (i + 1) * SUB - EDGE, at]
                tile = jnp.take_along_axis(tile, flip, axis=0, mode="promise_in_bounds")
                image[HALF - (i + 1) * SUB : HALF - i * SUB, to] = tile
        return [
            pltpu.make_async_copy(image.at[:, pl.ds(start, width)], out_hbm.at[:, pl.ds(start, width)], out_sem.at[start // LANES])
            for start, width in ([(starts[0], WIDE)] if starts[1] == starts[0] + LANES else [(s, LANES) for s in starts])
        ]

    even = times(whole(rows_c), whole(cols_a))
    odd = times(whole(rows_s), whole(cols_b))
    strip = times(whole(edge_r, 1), whole(plain_c)) + times(whole(edge_i, 1), whole(plain_s))
    out = stitch(even, odd, strip[:M], strip[M:], (LANES, 2 * LANES))
    for copy in out:
        copy.start()

    def outer(g, carry):
        columns(g, OUTER)
        edges(g, 0)
        edges(g, 2)
        return carry

    lax.fori_loop(0, GROUPS, outer, 0)

    column = lax.broadcasted_iota(i32, (1, WIDE), 1)
    column = jnp.where(column < LANES, column, column + C - WIDE).astype(f32)
    t_mid = jnp.minimum(jnp.minimum((column + (M + 0.5)) * (1 / (2 * M)), (C + M - 0.5 - column) * (1 / (2 * M))), 1.0)
    t_left = jnp.maximum(M - 0.5 - column, 0.0) * (1 / (2 * M))
    t_right = jnp.maximum(column - (C - M - 0.5), 0.0) * (1 / (2 * M))
    even = times(whole(rows_c), whole(cols_a))
    odd = times(whole(rows_s), whole(cols_b))
    strip = jnp.zeros((2 * M, WIDE), f32)
    for side, taper in ((0, t_left), (1, t_mid), (2, t_right)):
        strip = strip + (times(whole(edge_r, side), whole(plain_c)) + times(whole(edge_i, side), whole(plain_s))) * taper
    last = stitch(even, odd, strip[:M], strip[M:], (0, C - LANES))
    for copy in last:
        copy.start()
    for copy in out + last:
        copy.wait()


def image_of(uv, w):
    anywhere = pl.BlockSpec(memory_space=pl.ANY)
    f32, bf16 = jnp.float32, jnp.bfloat16
    return pl.pallas_call(
        image_kernel,
        out_shape=jax.ShapeDtypeStruct((R, C), f32),
        in_specs=[anywhere] * 2,
        out_specs=anywhere,
        scratch_shapes=[
            pltpu.VMEM((2, SUB, LANES), jnp.int32),
            pltpu.VMEM((18, SUB, LANES), f32),
            pltpu.VMEM((2, SUB, LANES), f32),
            pltpu.VMEM((2, GROUPS, SUB, LANES), f32),
            pltpu.VMEM((2, GROUPS, LOW, LANES), f32),
            pltpu.VMEM((GROUPS, HALF, LANES), bf16),
            pltpu.VMEM((GROUPS, HALF, LANES), bf16),
            pltpu.VMEM((GROUPS, WIDE, LANES), bf16),
            pltpu.VMEM((GROUPS, WIDE, LANES), bf16),
            pltpu.VMEM((GROUPS, WIDE, LANES), bf16),
            pltpu.VMEM((GROUPS, WIDE, LANES), bf16),
            pltpu.VMEM((3, GROUPS, 2 * M, LANES), bf16),
            pltpu.VMEM((3, GROUPS, 2 * M, LANES), bf16),
            pltpu.VMEM((R, C), f32),
            pltpu.SemaphoreType.DMA((2,)),
            pltpu.SemaphoreType.DMA((4,)),
        ],
        compiler_params=pltpu.CompilerParams(vmem_limit_bytes=56 * 1024 * 1024),
        name="image",
    )(uv, w)


def shards(vis, station_pairs, visibility_time_slot, station_u_cells, station_v_cells, facet_station_gains, holder_device_order):
    gains = facet_station_gains.reshape(2, GAIN_ROWS, LANES).transpose(1, 0, 2).reshape(2 * GAIN_ROWS, LANES)
    uv, w = exchange(
        holder_device_order, vis, station_pairs, visibility_time_slot.reshape(1, BLOCK),
        station_u_cells.reshape(4, LANES), station_v_cells.reshape(4, LANES), gains,
    )
    return image_of(uv, w)


def solution(mesh):
    return jax.shard_map(
        shards,
        mesh=mesh,
        in_specs=(
            P(None, ("frow", "fcol")),
            P(None, ("frow", "fcol")),
            P(("frow", "fcol")),
            P(),
            P(),
            P("frow", "fcol", None, None),
            P(),
        ),
        out_specs=P("frow", "fcol"),
        check_vma=False,
    )
```

time: 366 us -> 47 us (0.13)
  the two profiles are of different devices: /device:TPU:71 before, /device:TPU:39 now
where the time goes in v2:
time: 47 us; the launch traced here: 46.8 us
  Pallas kernels  46.7 us (99%)
    pallas_call x1, Pallas kernels, exchange(): pl.pallas_call(exchange_kernel, out_shape=(jax.ShapeDtypeStruct((2, SUB,...  38.5 us
    pallas_call x1, Pallas kernels, image_of(): pl.pallas_call(image_kernel, out_shape=jax.ShapeDtypeStruct((R, C), f32),...  8.25 us

profile of v2, /device:TPU:39, one launch (start us, length us, event | category | flops | bytes accessed | tf_op | source)
XLA Modules:
  0.0 46.8 jit_solution(2743898326006853206)
XLA Ops:
  0.0 38.5 %exchange.1 = (s32[2,8,128]{2,1,0:T(8,128)}, f32[18,8,128]{2,1,0:T(8,128)}) custom-call(s32[512]{0:T(512)} %order_hbm.1, f32[2,256]{1,0:T(2,128)} %vis_hbm.1, s32[2,256]{1,0:T(2,128)} %pairs_hbm.1, s32[1,256]{1,0:T(1,128)} %bitcast.11, s32[4,128]{1,0:T(4,128)} %bitcast.9, s32[4,128]{1,0:T(4,128)} %bitcast.10, f32[128,128]{1,0:T(8,128)} %bitcast.8), custom_call_target="tpu_custom_call" | custom-call | tf_op jit(solution)/shard_map/exchange/pallas_call | solution.py:276
  38.5 8.3 %image.1 = f32[1024,512]{1,0:T(8,128)} custom-call(s32[2,8,128]{2,1,0:T(8,128)} %get-tuple-element.7.uv_hbm, f32[18,8,128]{2,1,0:T(8,128)} %get-tuple-element.8.w_hbm), custom_call_target="tpu_custom_call" | custom-call | tf_op jit(solution)/shard_map/image/pallas_call | solution.py:482

commit v3 on v2

--- a/solution.py
+++ b/solution.py
@@ -51,13 +51,23 @@
     return jnp.take_along_axis(row, index, axis=1, mode="promise_in_bounds")
 
 
+HALF = R // 2
+LOW = 32
+WIDE = 256
+EDGE = HALF - M
+INNER = tuple(range(-4, 4))
+MARGIN = (-8, -7, 6, 7)
+OUTER = tuple(range(-8, -4)) + tuple(range(4, 8))
+
+
 def exchange_kernel(
-    order_hbm, vis_hbm, pairs_hbm, slot_hbm, ucell_hbm, vcell_hbm, gain_hbm, uv_ref, w_ref,
-    order, vis, pairs, slot, ucell, vcell, gain, pay, raw, part, line, done, w_own, w_all,
+    order_hbm, vis_hbm, pairs_hbm, slot_hbm, ucell_hbm, vcell_hbm, gain_hbm,
+    w_ref, wave_v, turn_v, rim_wave, rows_c, rows_s, cols_a, cols_b, plain_c, plain_s, centre, rim,
+    order, vis, pairs, slot, ucell, vcell, gain, pay, raw, part, line, done, w_own, w_all, uv_ref, turn_u,
     in_sem, send1, recv1, send2, recv2, send3, recv3, send_w, recv_w,
 ):
     fr, fc = lax.axis_index("frow"), lax.axis_index("fcol")
-    f32, i32 = jnp.float32, jnp.int32
+    f32, i32, bf16 = jnp.float32, jnp.int32, jnp.bfloat16
     z_lo, y = lax.div(fr, 4), lax.rem(fr, 4)
     z_hi, xc = lax.div(fc, 8), lax.rem(fc, 8)
     me = y * 8 + xc
@@ -241,90 +251,12 @@
 
     turn(4, w_own[0], w_own[1])
 
-    for j in range(PIECES):
-        @pl.when(me != 3 * j)
-        def _():
-            piece_copy(j).wait_send()
-
-    @pl.when(reduces)
-    def _():
-        for z in range(DEPTH):
-            @pl.when(my_z != z)
-            def _():
-                line_copy(z).wait_send()
-
-        for s in range(PLANE):
-            @pl.when(me != s)
-            def _():
-                done_copy(s).wait_send()
-
-    for dr, dc in AROUND:
-        @pl.when(inside(dr, dc))
-        def _():
-            weight_copy(dr, dc).wait_send()
-            slot_of = w_all.at[place(dr, dc)]
-            pltpu.make_async_copy(slot_of, slot_of, recv_w.at[place(dr, dc)]).wait()
-
-    for dr, dc in AROUND:
-        turn(place(dr, dc), w_all[place(dr, dc), 0], w_all[place(dr, dc), 1])
-
-
-def exchange(order, vis, pairs, slot, ucell, vcell, gain):
-    vmem = pl.BlockSpec(memory_space=pltpu.VMEM)
-    dma = pltpu.SemaphoreType.DMA
-    f32, i32 = jnp.float32, jnp.int32
-    return pl.pallas_call(
-        exchange_kernel,
-        out_shape=(jax.ShapeDtypeStruct((2, SUB, LANES), i32), jax.ShapeDtypeStruct((18, SUB, LANES), f32)),
-        in_specs=[pl.BlockSpec(memory_space=pl.ANY)] * 7,
-        out_specs=(vmem, vmem),
-        scratch_shapes=[
-            pltpu.SMEM((N_FROW * N_FCOL,), i32),
-            pltpu.VMEM((2, BLOCK), f32),
-            pltpu.VMEM((2, BLOCK), i32),
-            pltpu.VMEM((1, BLOCK), i32),
-            pltpu.VMEM((4, LANES), i32),
-            pltpu.VMEM((4, LANES), i32),
-            pltpu.VMEM((2 * GAIN_ROWS, LANES), f32),
-            pltpu.VMEM((PIECES, 1, LANES), f32),
-            pltpu.VMEM((PLANE, 1, LANES), f32),
-            pltpu.VMEM((NBLK, LANES), f32),
-            pltpu.VMEM((DEPTH, NBLK, LANES), f32),
-            pltpu.VMEM((PIECES, NBLK, LANES), f32),
-            pltpu.VMEM((2, SUB, LANES), f32),
-            pltpu.VMEM((9, 2, SUB, LANES), f32),
-            dma((7,)), dma((PIECES,)), dma, dma((DEPTH,)), dma, dma((PLANE,)), dma, dma((9,)), dma((9,)),
-        ],
-        compiler_params=pltpu.CompilerParams(collective_id=0, has_side_effects=True),
-        name="exchange",
-    )(order, vis, pairs, slot, ucell, vcell, gain)
-
-
-HALF = R // 2
-LOW = 32
-WIDE = 256
-EDGE = HALF - M
-INNER = tuple(range(-4, 4))
-OUTER = tuple(range(-8, -4)) + tuple(range(4, 8))
-
-
-def image_kernel(
-    uv_hbm, w_hbm, out_hbm,
-    uv_scr, w_scr, turn_u, turn_v, wave_v, rows_c, rows_s,
-    cols_a, cols_b, plain_c, plain_s, edge_r, edge_i, image, in_sem, out_sem,
-):
-    f32, i32, bf16 = jnp.float32, jnp.int32, jnp.bfloat16
-    loads = [pltpu.make_async_copy(uv_hbm, uv_scr, in_sem.at[0]), pltpu.make_async_copy(w_hbm, w_scr, in_sem.at[1])]
-    for load in loads:
-        load.start()
-    for load in loads:
-        load.wait()
     low = lax.broadcasted_iota(i32, (LOW, LANES), 0)
     step = lax.broadcasted_iota(i32, (SUB, LANES), 0) + 1
 
     def row_tables(g):
-        u = uv_scr[0, pl.ds(g, 1), :]
-        v = uv_scr[1, pl.ds(g, 1), :]
+        u = uv_ref[0, pl.ds(g, 1), :]
+        v = uv_ref[1, pl.ds(g, 1), :]
         lc, ls = circle(u * (2 * low + 1 + HALF))
         hc, hs = circle(u * (2 * LOW * step))
         turn_u[0] = hc
@@ -334,6 +266,9 @@
             at = slice((block + 8) * LOW, (block + 9) * LOW)
             rows_c[g, at, :] = c.astype(bf16)
             rows_s[g, at, :] = s.astype(bf16)
+            if block >= 6:
+                rim_wave[0, g, (block - 6) * LOW : (block - 5) * LOW, :] = c
+                rim_wave[1, g, (block - 6) * LOW : (block - 5) * LOW, :] = s
 
         put(0, lc, ls)
         for h in range(1, 9):
@@ -363,40 +298,138 @@
         return {h: (rc - ix, ic + rs), -h: (rc + ix, ic - rs)}
 
     def weighted(g, f, lc, ls):
-        w_r, w_i = w_scr[2 * f, pl.ds(g, 1), :], w_scr[2 * f + 1, pl.ds(g, 1), :]
+        w_r, w_i = w_ref[2 * f, pl.ds(g, 1), :], w_ref[2 * f + 1, pl.ds(g, 1), :]
         return w_r * lc - w_i * ls, w_r * ls + w_i * lc
 
-    def columns(g, blocks):
+    def keep(g, spot, block, own, plain):
+        at = slice(block * LOW, (block + 1) * LOW)
+        if own is not None:
+            cols_a[spot, g, at, :] = own[0].astype(bf16)
+            cols_b[spot, g, at, :] = own[1].astype(bf16)
+        if plain is not None:
+            plain_c[spot, g, at, :] = plain[0].astype(bf16)
+            plain_s[spot, g, at, :] = plain[1].astype(bf16)
+
+    def columns(g, spot):
+        blocks = (INNER, OUTER)[spot]
         lc, ls = wave_v[0, g], wave_v[1, g]
         z_r, z_i = weighted(g, 4, lc, ls)
         plain = {0: (lc, ls)}
         own = {0: (z_r, z_i)}
         for h in sorted({abs(b) for b in blocks} - {0}):
             plain.update(turned(g, h, lc, ls))
-            own.update(turned(g, h, z_r, z_i))
-        for f, side in ((3, [b for b in blocks if b < -6]), (5, [b for b in blocks if b > 5])):
-            if side:
-                s_r, s_i = weighted(g, f, lc, ls)
-                d_r, d_i = z_r - s_r, z_i - s_i
+            if h < 7:
+                own.update(turned(g, h, z_r, z_i))
+        for n, b in enumerate(blocks):
+            keep(g, spot, n, own[b] if -7 < b < 6 else None, plain[b])
+
+    def inner(g, carry):
+        columns(g, 0)
+        return carry
+
+    lax.fori_loop(0, GROUPS, inner, 0)
+
+    def whole(ref, at=None):
+        return jnp.concatenate([ref[g] if at is None else ref[at, g] for g in range(GROUPS)], 1)
+
+    def times(rows, cols):
+        return lax.dot_general(rows, cols, (((1,), (1,)), ((), ())), preferred_element_type=f32)
+
+    flip = SUB - 1 - lax.broadcasted_iota(i32, (SUB, LANES), 0)
+
+    def lay(even, odd):
+        down = even - odd
+        up = even + odd
+        rim[0] = up[EDGE:]
+        rim[1] = down[EDGE:]
+        centre[EDGE:, :] = down[:EDGE]
+        for i in range(EDGE // SUB):
+            for k in range(WIDE // LANES):
+                at = slice(k * LANES, (k + 1) * LANES)
+                tile = jnp.take_along_axis(up[i * SUB : (i + 1) * SUB, at], flip, axis=0, mode="promise_in_bounds")
+                centre[EDGE - (i + 1) * SUB : EDGE - i * SUB, at] = tile
+
+    lay(times(whole(rows_c), whole(cols_a, 0)), times(whole(rows_s), whole(cols_b, 0)))
+    for g in range(GROUPS):
+        columns(g, 1)
+
+    for j in range(PIECES):
+        @pl.when(me != 3 * j)
+        def _():
+            piece_copy(j).wait_send()
+
+    @pl.when(reduces)
+    def _():
+        for z in range(DEPTH):
+            @pl.when(my_z != z)
+            def _():
+                line_copy(z).wait_send()
+
+        for s in range(PLANE):
+            @pl.when(me != s)
+            def _():
+                done_copy(s).wait_send()
+
+    for dr, dc in AROUND:
+        @pl.when(inside(dr, dc))
+        def _():
+            weight_copy(dr, dc).wait_send()
+            slot_of = w_all.at[place(dr, dc)]
+            pltpu.make_async_copy(slot_of, slot_of, recv_w.at[place(dr, dc)]).wait()
+
+    for dr, dc in AROUND:
+        turn(place(dr, dc), w_all[place(dr, dc), 0], w_all[place(dr, dc), 1])
+
+
+def image_kernel(
+    w_ref, wave_v, turn_v, rim_wave, rows_c, rows_s, cols_a, cols_b, plain_c, plain_s, centre, rim, out_hbm,
+    edge_a, edge_b, edge_r, edge_i, image, out_sem,
+):
+    f32, i32, bf16 = jnp.float32, jnp.int32, jnp.bfloat16
+
+    def store(n, source, rows, cols):
+        copy = pltpu.make_async_copy(source, out_hbm.at[pl.ds(*rows), pl.ds(*cols)], out_sem.at[n])
+        copy.start()
+        return copy
+
+    stores = [store(0, centre, (M, 2 * EDGE), (LANES, WIDE))]
+    low = lax.broadcasted_iota(i32, (LOW, LANES), 0)
+    lowf = low.astype(f32)
+
+    def turned(g, h, real, imag):
+        bc, bs = turn_v[0, g, h - 1 : h, :], turn_v[1, g, h - 1 : h, :]
+        rc, ix, rs, ic = real * bc, imag * bs, real * bs, imag * bc
+        return {h: (rc - ix, ic + rs), -h: (rc + ix, ic - rs)}
+
+    def weighted(g, f, lc, ls):
+        w_r, w_i = w_ref[2 * f, pl.ds(g, 1), :], w_ref[2 * f + 1, pl.ds(g, 1), :]
+        return w_r * lc - w_i * ls, w_r * ls + w_i * lc
+
+    def keep(g, block, own):
+        at = slice(block * LOW, (block + 1) * LOW)
+        edge_a[g, at, :] = own[0].astype(bf16)
+        edge_b[g, at, :] = own[1].astype(bf16)
+
+    def shared(g):
+        lc, ls = wave_v[0, g], wave_v[1, g]
+        z_r, z_i = weighted(g, 4, lc, ls)
+        for f, side in ((3, (-8, -7)), (5, (6, 7))):
+            s_r, s_i = weighted(g, f, lc, ls)
+            d_r, d_i = z_r - s_r, z_i - s_i
             for b in side:
                 start = (b + 8) * LOW
                 if b < 0:
                     taper = (lowf + (start + M + 0.5)) * (1 / (2 * M))
                 else:
                     taper = (C + M - 0.5 - start - lowf) * (1 / (2 * M))
-                own[b] = turned(g, abs(b), s_r + taper * d_r, s_i + taper * d_i)[b]
-        for n, b in enumerate(blocks):
-            at = slice(n * LOW, (n + 1) * LOW)
-            for refs, values in (((cols_a, cols_b), own[b]), ((plain_c, plain_s), plain[b])):
-                refs[0][g, at, :] = values[0].astype(bf16)
-                refs[1][g, at, :] = values[1].astype(bf16)
+                keep(g, MARGIN.index(b), turned(g, abs(b), s_r + taper * d_r, s_i + taper * d_i)[b])
 
     def edges(g, side):
-        u = uv_scr[0, pl.ds(g, 1), :]
         for half in range(M // LOW):
-            c, s = edge_wave(g, u, half)
+            at_half = slice(half * LOW, (half + 1) * LOW)
+            c, s = rim_wave[0, g, at_half, :], rim_wave[1, g, at_half, :]
             for f, sign, at in ((side, -1.0, half * LOW), (6 + side, 1.0, M + half * LOW)):
-                w_r, w_i = w_scr[2 * f, pl.ds(g, 1), :], w_scr[2 * f + 1, pl.ds(g, 1), :]
+                w_r, w_i = w_ref[2 * f, pl.ds(g, 1), :], w_ref[2 * f + 1, pl.ds(g, 1), :]
                 if sign > 0:
                     real, minus = w_r * c - w_i * s, w_r * s + w_i * c
                 else:
@@ -404,16 +437,6 @@
                 edge_r[side, g, at : at + LOW, :] = real.astype(bf16)
                 edge_i[side, g, at : at + LOW, :] = (-minus).astype(bf16)
 
-    def edge_wave(g, u, half):
-        return circle(u * (2 * low + 1 + 2 * (EDGE + half * LOW)))
-
-    def inner(g, carry):
-        columns(g, INNER)
-        edges(g, 1)
-        return carry
-
-    lax.fori_loop(0, GROUPS, inner, 0)
-
     def whole(ref, at=None):
         return jnp.concatenate([ref[g] if at is None else ref[at, g] for g in range(GROUPS)], 1)
 
@@ -425,95 +448,135 @@
     t_next = (d + 0.5) * (1 / (2 * M))
     flip = SUB - 1 - lax.broadcasted_iota(i32, (SUB, LANES), 0)
 
-    def stitch(even, odd, above, below, starts):
-        down = even - odd
-        up = even + odd
-        low_edge = down[EDGE:] * t_own + below * t_next
-        high_edge = up[EDGE:] * t_own + above * t_next
-        for k, start in enumerate(starts):
-            at = slice(k * LANES, (k + 1) * LANES)
-            to = slice(start, start + LANES)
-            image[HALF : R - M, to] = down[:EDGE, at]
-            image[R - M :, to] = low_edge[:, at]
-            for i in range(HALF // SUB):
-                tile = up[i * SUB : (i + 1) * SUB, at] if i < EDGE // SUB else high_edge[i * SUB - EDGE : (i + 1) * SUB - EDGE, at]
-                tile = jnp.take_along_axis(tile, flip, axis=0, mode="promise_in_bounds")
-                image[HALF - (i + 1) * SUB : HALF - i * SUB, to] = tile
-        return [
-            pltpu.make_async_copy(image.at[:, pl.ds(start, width)], out_hbm.at[:, pl.ds(start, width)], out_sem.at[start // LANES])
-            for start, width in ([(starts[0], WIDE)] if starts[1] == starts[0] + LANES else [(s, LANES) for s in starts])
-        ]
-
-    even = times(whole(rows_c), whole(cols_a))
-    odd = times(whole(rows_s), whole(cols_b))
-    strip = times(whole(edge_r, 1), whole(plain_c)) + times(whole(edge_i, 1), whole(plain_s))
-    out = stitch(even, odd, strip[:M], strip[M:], (LANES, 2 * LANES))
-    for copy in out:
-        copy.start()
-
-    def outer(g, carry):
-        columns(g, OUTER)
-        edges(g, 0)
-        edges(g, 2)
+    def lay(down, up, start):
+        to = slice(start, start + LANES)
+        image[HALF : R - M, to] = down[:EDGE]
+        for i in range(EDGE // SUB):
+            tile = jnp.take_along_axis(up[i * SUB : (i + 1) * SUB], flip, axis=0, mode="promise_in_bounds")
+            image[HALF - (i + 1) * SUB : HALF - i * SUB, to] = tile
+
+    def seam(up, down, strip, start):
+        to = slice(start, start + LANES)
+        top = up * t_own + strip[:M] * t_next
+        image[R - M :, to] = down * t_own + strip[M:] * t_next
+        for i in range(M // SUB):
+            tile = jnp.take_along_axis(top[i * SUB : (i + 1) * SUB], flip, axis=0, mode="promise_in_bounds")
+            image[M - (i + 1) * SUB : M - i * SUB, to] = tile
+
+    def rest(g, carry):
+        shared(g)
+        for side in range(3):
+            edges(g, side)
         return carry
 
-    lax.fori_loop(0, GROUPS, outer, 0)
+    lax.fori_loop(0, GROUPS, rest, 0)
 
     column = lax.broadcasted_iota(i32, (1, WIDE), 1)
     column = jnp.where(column < LANES, column, column + C - WIDE).astype(f32)
     t_mid = jnp.minimum(jnp.minimum((column + (M + 0.5)) * (1 / (2 * M)), (C + M - 0.5 - column) * (1 / (2 * M))), 1.0)
     t_left = jnp.maximum(M - 0.5 - column, 0.0) * (1 / (2 * M))
     t_right = jnp.maximum(column - (C - M - 0.5), 0.0) * (1 / (2 * M))
-    even = times(whole(rows_c), whole(cols_a))
-    odd = times(whole(rows_s), whole(cols_b))
-    strip = jnp.zeros((2 * M, WIDE), f32)
-    for side, taper in ((0, t_left), (1, t_mid), (2, t_right)):
-        strip = strip + (times(whole(edge_r, side), whole(plain_c)) + times(whole(edge_i, side), whole(plain_s))) * taper
-    last = stitch(even, odd, strip[:M], strip[M:], (0, C - LANES))
-    for copy in last:
-        copy.start()
-    for copy in out + last:
+
+    def strip_of(side, spot):
+        return times(whole(edge_r, side), whole(plain_c, spot)) + times(whole(edge_i, side), whole(plain_s, spot))
+
+    def outer_cols(inner_ref, edge_ref):
+        parts = []
+        for g in range(GROUPS):
+            own = inner_ref[1, g]
+            parts.append(jnp.concatenate([edge_ref[g, : 2 * LOW], own[2 * LOW : 6 * LOW], edge_ref[g, 2 * LOW :]], 0))
+        return jnp.concatenate(parts, 1)
+
+    even = times(whole(rows_c), outer_cols(cols_a, edge_a))
+    odd = times(whole(rows_s), outer_cols(cols_b, edge_b))
+    down, up = even - odd, even + odd
+    for k, start in ((0, 0), (1, C - LANES)):
+        at = slice(k * LANES, (k + 1) * LANES)
+        lay(down[:EDGE, at], up[:EDGE, at], start)
+        stores.append(store(1 + k, image.at[pl.ds(M, 2 * EDGE), pl.ds(start, LANES)], (M, 2 * EDGE), (start, LANES)))
+    strip = strip_of(1, 0)
+    for k in range(2):
+        at = slice(k * LANES, (k + 1) * LANES)
+        seam(rim[0, :, at], rim[1, :, at], strip[:, at], (k + 1) * LANES)
+    strip = strip_of(0, 1) * t_left + strip_of(1, 1) * t_mid + strip_of(2, 1) * t_right
+    for k, start in ((0, 0), (1, C - LANES)):
+        at = slice(k * LANES, (k + 1) * LANES)
+        seam(up[EDGE:, at], down[EDGE:, at], strip[:, at], start)
+    for n, row in ((3, 0), (4, R - M)):
+        stores.append(store(n, image.at[pl.ds(row, M)], (row, M), (0, C)))
+    for copy in stores:
         copy.wait()
 
 
-def image_of(uv, w):
-    anywhere = pl.BlockSpec(memory_space=pl.ANY)
-    f32, bf16 = jnp.float32, jnp.bfloat16
+def tile_of(order, vis, pairs, slot, ucell, vcell, gain):
+    dma, vmem = pltpu.SemaphoreType.DMA, pltpu.VMEM
+    f32, i32, bf16 = jnp.float32, jnp.int32, jnp.bfloat16
+    inside = pl.BlockSpec(memory_space=pltpu.VMEM)
+    kept = (
+        vmem((18, SUB, LANES), f32),
+        vmem((2, GROUPS, LOW, LANES), f32),
+        vmem((2, GROUPS, SUB, LANES), f32),
+        vmem((2, GROUPS, M, LANES), f32),
+        vmem((GROUPS, HALF, LANES), bf16),
+        vmem((GROUPS, HALF, LANES), bf16),
+        vmem((2, GROUPS, WIDE, LANES), bf16),
+        vmem((2, GROUPS, WIDE, LANES), bf16),
+        vmem((2, GROUPS, WIDE, LANES), bf16),
+        vmem((2, GROUPS, WIDE, LANES), bf16),
+        vmem((2 * EDGE, WIDE), f32),
+        vmem((2, M, WIDE), f32),
+    )
+    tables = pl.pallas_call(
+        exchange_kernel,
+        out_shape=kept,
+        in_specs=[pl.BlockSpec(memory_space=pltpu.HBM)] * 7,
+        out_specs=(inside,) * len(kept),
+        scratch_shapes=[
+            pltpu.SMEM((N_FROW * N_FCOL,), i32),
+            vmem((2, BLOCK), f32),
+            vmem((2, BLOCK), i32),
+            vmem((1, BLOCK), i32),
+            vmem((4, LANES), i32),
+            vmem((4, LANES), i32),
+            vmem((2 * GAIN_ROWS, LANES), f32),
+            vmem((PIECES, 1, LANES), f32),
+            vmem((PLANE, 1, LANES), f32),
+            vmem((NBLK, LANES), f32),
+            vmem((DEPTH, NBLK, LANES), f32),
+            vmem((PIECES, NBLK, LANES), f32),
+            vmem((2, SUB, LANES), f32),
+            vmem((9, 2, SUB, LANES), f32),
+            vmem((2, SUB, LANES), i32),
+            vmem((2, SUB, LANES), f32),
+            dma((7,)), dma((PIECES,)), dma, dma((DEPTH,)), dma, dma((PLANE,)), dma, dma((9,)), dma((9,)),
+        ],
+        compiler_params=pltpu.CompilerParams(collective_id=0, has_side_effects=True, vmem_limit_bytes=24 * 1024 * 1024),
+        name="exchange",
+    )(*[pltpu.with_memory_space_constraint(x, pltpu.HBM) for x in (order, vis, pairs, slot, ucell, vcell, gain)])
     return pl.pallas_call(
         image_kernel,
         out_shape=jax.ShapeDtypeStruct((R, C), f32),
-        in_specs=[anywhere] * 2,
-        out_specs=anywhere,
+        in_specs=[inside] * len(kept),
+        out_specs=pl.BlockSpec(memory_space=pl.ANY),
         scratch_shapes=[
-            pltpu.VMEM((2, SUB, LANES), jnp.int32),
-            pltpu.VMEM((18, SUB, LANES), f32),
-            pltpu.VMEM((2, SUB, LANES), f32),
-            pltpu.VMEM((2, GROUPS, SUB, LANES), f32),
-            pltpu.VMEM((2, GROUPS, LOW, LANES), f32),
-            pltpu.VMEM((GROUPS, HALF, LANES), bf16),
-            pltpu.VMEM((GROUPS, HALF, LANES), bf16),
-            pltpu.VMEM((GROUPS, WIDE, LANES), bf16),
-            pltpu.VMEM((GROUPS, WIDE, LANES), bf16),
-            pltpu.VMEM((GROUPS, WIDE, LANES), bf16),
-            pltpu.VMEM((GROUPS, WIDE, LANES), bf16),
-            pltpu.VMEM((3, GROUPS, 2 * M, LANES), bf16),
-            pltpu.VMEM((3, GROUPS, 2 * M, LANES), bf16),
-            pltpu.VMEM((R, C), f32),
-            pltpu.SemaphoreType.DMA((2,)),
-            pltpu.SemaphoreType.DMA((4,)),
+            vmem((GROUPS, 2 * M, LANES), bf16),
+            vmem((GROUPS, 2 * M, LANES), bf16),
+            vmem((3, GROUPS, 2 * M, LANES), bf16),
+            vmem((3, GROUPS, 2 * M, LANES), bf16),
+            vmem((R, C), f32),
+            dma((5,)),
         ],
-        compiler_params=pltpu.CompilerParams(vmem_limit_bytes=56 * 1024 * 1024),
+        compiler_params=pltpu.CompilerParams(vmem_limit_bytes=24 * 1024 * 1024),
         name="image",
-    )(uv, w)
+    )(*tables)
 
 
 def shards(vis, station_pairs, visibility_time_slot, station_u_cells, station_v_cells, facet_station_gains, holder_device_order):
     gains = facet_station_gains.reshape(2, GAIN_ROWS, LANES).transpose(1, 0, 2).reshape(2 * GAIN_ROWS, LANES)
-    uv, w = exchange(
+    return tile_of(
         holder_device_order, vis, station_pairs, visibility_time_slot.reshape(1, BLOCK),
         station_u_cells.reshape(4, LANES), station_v_cells.reshape(4, LANES), gains,
     )
-    return image_of(uv, w)
 
 
 def solution(mesh):

time: 47 us -> 41.6 us (0.89)
  Pallas kernels: 46.7 us -> 41.5 us
    pallas_call x2, Pallas kernels: 46.7 us -> 41.5 us  [the longest x1 37.9 us: tile_of(): pl.pallas_call(exchange_kernel, out_shape=kept, in_specs=[pl.BlockSpec(me...]
where the time goes in v3:
time: 41.6 us; the launch traced here: 41.5 us
  Pallas kernels  41.5 us (100%)
    pallas_call x1, Pallas kernels, tile_of(): pl.pallas_call(exchange_kernel, out_shape=kept, in_specs=[pl.BlockSpec(me...  37.9 us
    pallas_call x1, Pallas kernels, tile_of(): pl.pallas_call(image_kernel, out_shape=jax.ShapeDtypeStruct((R, C), f32),...  3.61 us

profile of v3, /device:TPU:39, one launch (start us, length us, event | category | flops | bytes accessed | tf_op | source)
XLA Modules:
  0.0 41.5 jit_solution(7758110625911079037)
XLA Ops:
  0.0 37.9 %exchange.1 = (f32[18,8,128]{2,1,0:T(8,128)S(1)}, f32[2,8,32,128]{3,2,1,0:T(8,128)S(1)}, f32[2,8,8,128]{3,2,1,0:T(8,128)S(1)}, f32[2,8,64,128]{3,2,1,0:T(8,128)S...) custom-call(s32[512]{0:T(512)} %order_hbm.1, ...), custom_call_target="tpu_custom_call" | custom-call | tf_op jit(solution)/shard_map/exchange/pallas_call | solution.py:529
  37.9 3.6 %image.1 = f32[1024,512]{1,0:T(8,128)} custom-call(f32[18,8,128]{2,1,0:T(8,128)S(1)} %get-tuple-element.17.w_ref, f32[2,8,32,128]{3,2,1,0:T(8,128)S(1)} %get-tuple-element.18.wave_v, f32[2,8,8,128]{3,2,1,0:T(8,128)S(1)} %get-tuple-element.19.turn_v, f32[2,8,64,128]{3,2,1,0:T(8,128)S(1)} %get-tuple-element.20.rim_wave, ...), custom_call_target="tpu_custom_call" | custom-call | tf_op jit(solution)/shard_map/image/pallas_call | solution.py:556

commit v4 on v3

--- a/solution.py
+++ b/solution.py
@@ -23,6 +23,8 @@
 PLANE = 32
 DEPTH = 16
 PIECES = 10
+REDUCERS = tuple(6 * (j // 2) + j % 2 for j in range(PIECES))
+PEERS = REDUCERS + tuple(s for s in range(PLANE) if s not in REDUCERS)
 GAIN_ROWS = 64
 MESH = pl.DeviceIdType.MESH
 AROUND = [(dr, dc) for dr in (-1, 0, 1) for dc in (-1, 0, 1) if (dr, dc) != (0, 0)]
@@ -63,7 +65,7 @@
 def exchange_kernel(
     order_hbm, vis_hbm, pairs_hbm, slot_hbm, ucell_hbm, vcell_hbm, gain_hbm,
     w_ref, wave_v, turn_v, rim_wave, rows_c, rows_s, cols_a, cols_b, plain_c, plain_s, centre, rim,
-    order, vis, pairs, slot, ucell, vcell, gain, pay, raw, part, line, done, w_own, w_all, uv_ref, turn_u,
+    order, vis, pairs, slot, ucell, vcell, gain, pay, raw, part, line, done, w_own, w_all, uv_ref, turn_u, spin,
     in_sem, send1, recv1, send2, recv2, send3, recv3, send_w, recv_w,
 ):
     fr, fc = lax.axis_index("frow"), lax.axis_index("fcol")
@@ -72,8 +74,8 @@
     z_hi, xc = lax.div(fc, 8), lax.rem(fc, 8)
     me = y * 8 + xc
     my_z = z_hi * 4 + z_lo
-    mine = lax.div(me, 3)
-    reduces = jnp.logical_and(lax.rem(me, 3) == 0, mine < PIECES)
+    mine = 2 * lax.div(me, 6) + lax.rem(me, 6)
+    reduces = jnp.logical_and(lax.rem(me, 6) < 2, mine < PIECES)
     plane_row, plane_col = z_lo * 4, z_hi * 8
 
     def in_plane(s):
@@ -86,6 +88,10 @@
         row, col = fr + dr, fc + dc
         return (row >= 0) & (row < N_FROW) & (col >= 0) & (col < N_FCOL)
 
+    loads = ((vis_hbm, vis), (pairs_hbm, pairs), (slot_hbm, slot), (order_hbm, order), (ucell_hbm, ucell), (vcell_hbm, vcell), (gain_hbm, gain))
+    loads = [pltpu.make_async_copy(a, b, in_sem.at[n]) for n, (a, b) in enumerate(loads)]
+    for load in loads[:4]:
+        load.start()
     barrier = pltpu.get_barrier_semaphore()
 
     def greet(device):
@@ -106,7 +112,7 @@
     @pl.when(jnp.logical_not(reduces))
     def _():
         for j in range(PIECES):
-            greet(in_plane(3 * j))
+            greet(in_plane(REDUCERS[j]))
 
     count = jnp.where(reduces, PLANE - 1 + DEPTH - 1, PIECES)
     for dr, dc in AROUND:
@@ -116,16 +122,14 @@
         def _():
             greet((fr + dr, fc + dc))
 
-    loads = ((vis_hbm, vis), (pairs_hbm, pairs), (slot_hbm, slot), (order_hbm, order), (ucell_hbm, ucell), (vcell_hbm, vcell), (gain_hbm, gain))
-    loads = [pltpu.make_async_copy(a, b, in_sem.at[n]) for n, (a, b) in enumerate(loads)]
-    for load in loads:
+    for load in loads[4:]:
         load.start()
     for dr, dc in AROUND:
         @pl.when(jnp.logical_not(inside(dr, dc)))
         def _():
             w_all[place(dr, dc)] = jnp.zeros((2, SUB, LANES), f32)
 
-    for load in loads:
+    for load in loads[:4]:
         load.wait()
     for half in range(2):
         cols = slice(half * LANES, (half + 1) * LANES)
@@ -140,7 +144,7 @@
     def piece_copy(j):
         return pltpu.make_async_remote_copy(
             src_ref=pay.at[j], dst_ref=raw.at[me], send_sem=send1.at[j], recv_sem=recv1,
-            device_id=in_plane(3 * j), device_id_type=MESH,
+            device_id=in_plane(REDUCERS[j]), device_id_type=MESH,
         )
 
     def line_copy(z):
@@ -167,7 +171,7 @@
         pltpu.make_async_copy(view, view, sem).wait()
 
     for j in range(PIECES):
-        @pl.when(me != 3 * j)
+        @pl.when(me != REDUCERS[j])
         def _():
             piece_copy(j).start()
 
@@ -188,7 +192,7 @@
         line[my_z] = part[...]
         landed(line, DEPTH - 1, recv2)
         done[mine] = jnp.sum(line[...], axis=0)
-        for s in range(PLANE):
+        for s in PEERS:
             @pl.when(me != s)
             def _():
                 done_copy(s).start()
@@ -198,6 +202,9 @@
     @pl.when(jnp.logical_not(reduces))
     def _():
         landed(done, PIECES, recv3)
+
+    for load in loads[4:]:
+        load.wait()
 
     def value(v):
         return jnp.concatenate([done[2 * v], done[2 * v + 1]], 0)
@@ -254,10 +261,22 @@
     low = lax.broadcasted_iota(i32, (LOW, LANES), 0)
     step = lax.broadcasted_iota(i32, (SUB, LANES), 0) + 1
 
+    for n, cells in enumerate((uv_ref[0], uv_ref[1])):
+        for i in range(1, LOW // SUB):
+            spin[n, i - 1, 0], spin[n, i - 1, 1] = circle(cells * (2 * SUB * i))
+
+    def fan(n, g, c, s):
+        cos, sin = [c], [s]
+        for i in range(LOW // SUB - 1):
+            bc, bs = spin[n, i, 0, pl.ds(g, 1), :], spin[n, i, 1, pl.ds(g, 1), :]
+            cos.append(c * bc - s * bs)
+            sin.append(s * bc + c * bs)
+        return jnp.concatenate(cos, 0), jnp.concatenate(sin, 0)
+
     def row_tables(g):
         u = uv_ref[0, pl.ds(g, 1), :]
         v = uv_ref[1, pl.ds(g, 1), :]
-        lc, ls = circle(u * (2 * low + 1 + HALF))
+        lc, ls = fan(0, g, *circle(u * (2 * step - 1 + HALF)))
         hc, hs = circle(u * (2 * LOW * step))
         turn_u[0] = hc
         turn_u[1] = hs
@@ -277,7 +296,7 @@
             put(-h, cc + ss, sc - cs)
             if h < 8:
                 put(h, cc - ss, sc + cs)
-        lc, ls = circle(v * (2 * low))
+        lc, ls = fan(1, g, *circle(v * (2 * step - 2)))
         wave_v[0, g] = lc
         wave_v[1, g] = ls
         hc, hs = circle(v * (2 * LOW * step))
@@ -354,7 +373,7 @@
         columns(g, 1)
 
     for j in range(PIECES):
-        @pl.when(me != 3 * j)
+        @pl.when(me != REDUCERS[j])
         def _():
             piece_copy(j).wait_send()
 
@@ -431,11 +450,11 @@
             for f, sign, at in ((side, -1.0, half * LOW), (6 + side, 1.0, M + half * LOW)):
                 w_r, w_i = w_ref[2 * f, pl.ds(g, 1), :], w_ref[2 * f + 1, pl.ds(g, 1), :]
                 if sign > 0:
-                    real, minus = w_r * c - w_i * s, w_r * s + w_i * c
+                    real, imag = w_r * c - w_i * s, w_r * s + w_i * c
                 else:
-                    real, minus = w_r * c + w_i * s, w_i * c - w_r * s
+                    real, imag = w_r * c + w_i * s, w_i * c - w_r * s
                 edge_r[side, g, at : at + LOW, :] = real.astype(bf16)
-                edge_i[side, g, at : at + LOW, :] = (-minus).astype(bf16)
+                edge_i[side, g, at : at + LOW, :] = imag.astype(bf16)
 
     def whole(ref, at=None):
         return jnp.concatenate([ref[g] if at is None else ref[at, g] for g in range(GROUPS)], 1)
@@ -463,13 +482,10 @@
             tile = jnp.take_along_axis(top[i * SUB : (i + 1) * SUB], flip, axis=0, mode="promise_in_bounds")
             image[M - (i + 1) * SUB : M - i * SUB, to] = tile
 
-    def rest(g, carry):
+    for g in range(GROUPS):
         shared(g)
         for side in range(3):
             edges(g, side)
-        return carry
-
-    lax.fori_loop(0, GROUPS, rest, 0)
 
     column = lax.broadcasted_iota(i32, (1, WIDE), 1)
     column = jnp.where(column < LANES, column, column + C - WIDE).astype(f32)
@@ -477,8 +493,10 @@
     t_left = jnp.maximum(M - 0.5 - column, 0.0) * (1 / (2 * M))
     t_right = jnp.maximum(column - (C - M - 0.5), 0.0) * (1 / (2 * M))
 
-    def strip_of(side, spot):
-        return times(whole(edge_r, side), whole(plain_c, spot)) + times(whole(edge_i, side), whole(plain_s, spot))
+    def strips(sides, spot):
+        real = jnp.concatenate([whole(edge_r, side) for side in sides], 0)
+        imag = jnp.concatenate([whole(edge_i, side) for side in sides], 0)
+        return times(real, whole(plain_c, spot)) - times(imag, whole(plain_s, spot))
 
     def outer_cols(inner_ref, edge_ref):
         parts = []
@@ -494,11 +512,12 @@
         at = slice(k * LANES, (k + 1) * LANES)
         lay(down[:EDGE, at], up[:EDGE, at], start)
         stores.append(store(1 + k, image.at[pl.ds(M, 2 * EDGE), pl.ds(start, LANES)], (M, 2 * EDGE), (start, LANES)))
-    strip = strip_of(1, 0)
+    strip = strips((1,), 0)
     for k in range(2):
         at = slice(k * LANES, (k + 1) * LANES)
         seam(rim[0, :, at], rim[1, :, at], strip[:, at], (k + 1) * LANES)
-    strip = strip_of(0, 1) * t_left + strip_of(1, 1) * t_mid + strip_of(2, 1) * t_right
+    strip = strips((0, 1, 2), 1)
+    strip = strip[: 2 * M] * t_left + strip[2 * M : 4 * M] * t_mid + strip[4 * M :] * t_right
     for k, start in ((0, 0), (1, C - LANES)):
         at = slice(k * LANES, (k + 1) * LANES)
         seam(up[EDGE:, at], down[EDGE:, at], strip[:, at], start)
@@ -548,6 +567,7 @@
             vmem((9, 2, SUB, LANES), f32),
             vmem((2, SUB, LANES), i32),
             vmem((2, SUB, LANES), f32),
+            vmem((2, LOW // SUB - 1, 2, SUB, LANES), f32),
             dma((7,)), dma((PIECES,)), dma, dma((DEPTH,)), dma, dma((PLANE,)), dma, dma((9,)), dma((9,)),
         ],
         compiler_params=pltpu.CompilerParams(collective_id=0, has_side_effects=True, vmem_limit_bytes=24 * 1024 * 1024),

time: 41.6 us -> 40.3 us (0.969)
  Pallas kernels: 41.5 us -> 40.2 us
    pallas_call x1, Pallas kernels: 3.61 us -> 2.47 us  [tile_of(): pl.pallas_call(image_kernel, out_shape=jax.ShapeDtypeStruct((R, C), f32),...]
where the time goes in v4:
time: 40.3 us; the launch traced here: 40.2 us
  Pallas kernels  40.2 us (100%)
    pallas_call x1, Pallas kernels, tile_of(): pl.pallas_call(exchange_kernel, out_shape=kept, in_specs=[pl.BlockSpec(me...  37.7 us
    pallas_call x1, Pallas kernels, tile_of(): pl.pallas_call(image_kernel, out_shape=jax.ShapeDtypeStruct((R, C), f32),...  2.47 us

profile of v4, /device:TPU:39, one launch (start us, length us, event | category | flops | bytes accessed | tf_op | source)
XLA Modules:
  0.0 40.2 jit_solution(9394796845039512145)
XLA Ops:
  0.0 37.7 %exchange.1 = (f32[18,8,128]{2,1,0:T(8,128)S(1)}, f32[2,8,32,128]{3,2,1,0:T(8,128)S(1)}, f32[2,8,8,128]{3,2,1,0:T(8,128)S(1)}, f32[2,8,64,128]{3,2,1,0:T(8,128)S...) custom-call(s32[512]{0:T(512)} %order_hbm.1, ...), custom_call_target="tpu_custom_call" | custom-call | tf_op jit(solution)/shard_map/exchange/pallas_call | solution.py:548
  37.7 2.5 %image.1 = f32[1024,512]{1,0:T(8,128)} custom-call(f32[18,8,128]{2,1,0:T(8,128)S(1)} %get-tuple-element.17.w_ref, f32[2,8,32,128]{3,2,1,0:T(8,128)S(1)} %get-tuple-element.18.wave_v, f32[2,8,8,128]{3,2,1,0:T(8,128)S(1)} %get-tuple-element.19.turn_v, f32[2,8,64,128]{3,2,1,0:T(8,128)S(1)} %get-tuple-element.20.rim_wave, ...), custom_call_target="tpu_custom_call" | custom-call | tf_op jit(solution)/shard_map/image/pallas_call | solution.py:576

commit v5 on v4

--- a/solution.py
+++ b/solution.py
@@ -27,7 +27,9 @@
 PEERS = REDUCERS + tuple(s for s in range(PLANE) if s not in REDUCERS)
 GAIN_ROWS = 64
 MESH = pl.DeviceIdType.MESH
-AROUND = [(dr, dc) for dr in (-1, 0, 1) for dc in (-1, 0, 1) if (dr, dc) != (0, 0)]
+NEAR = [(-1, 0), (1, 0)]
+FAR = [(dr, dc) for dc in (-1, 1) for dr in (-1, 1, 0)]
+AROUND = FAR + NEAR
 
 
 def place(dr, dc):
@@ -64,8 +66,8 @@
 
 def exchange_kernel(
     order_hbm, vis_hbm, pairs_hbm, slot_hbm, ucell_hbm, vcell_hbm, gain_hbm,
-    w_ref, wave_v, turn_v, rim_wave, rows_c, rows_s, cols_a, cols_b, plain_c, plain_s, centre, rim,
-    order, vis, pairs, slot, ucell, vcell, gain, pay, raw, part, line, done, w_own, w_all, uv_ref, turn_u, spin,
+    w_ref, wave_v, turn_v, rim_wave, rows_c, rows_s, cols_a, cols_b, plain_c, plain_s, centre, edge_r, edge_i,
+    order, vis, pairs, slot, ucell, vcell, gain, pay, raw, part, line, done, w_own, w_all, uv_ref, turn_u, spin, rim,
     in_sem, send1, recv1, send2, recv2, send3, recv3, send_w, recv_w,
 ):
     fr, fc = lax.axis_index("frow"), lax.axis_index("fcol")
@@ -356,21 +358,58 @@
 
     flip = SUB - 1 - lax.broadcasted_iota(i32, (SUB, LANES), 0)
 
+    d = lax.broadcasted_iota(i32, (M, 1), 0).astype(f32)
+    t_own = (2 * M - 0.5 - d) * (1 / (2 * M))
+    t_next = (d + 0.5) * (1 / (2 * M))
+    def edges(g, side):
+        for half in range(M // LOW):
+            at_half = slice(half * LOW, (half + 1) * LOW)
+            c, s = rim_wave[0, g, at_half, :], rim_wave[1, g, at_half, :]
+            for f, sign, at in ((side, -1.0, half * LOW), (6 + side, 1.0, M + half * LOW)):
+                w_r, w_i = w_ref[2 * f, pl.ds(g, 1), :], w_ref[2 * f + 1, pl.ds(g, 1), :]
+                if sign > 0:
+                    real, imag = w_r * c - w_i * s, w_r * s + w_i * c
+                else:
+                    real, imag = w_r * c + w_i * s, w_i * c - w_r * s
+                edge_r[g, at : at + LOW, :] = real.astype(bf16)
+                edge_i[g, at : at + LOW, :] = imag.astype(bf16)
+
     def lay(even, odd):
         down = even - odd
         up = even + odd
         rim[0] = up[EDGE:]
         rim[1] = down[EDGE:]
-        centre[EDGE:, :] = down[:EDGE]
+        centre[HALF : R - M, :] = down[:EDGE]
         for i in range(EDGE // SUB):
             for k in range(WIDE // LANES):
                 at = slice(k * LANES, (k + 1) * LANES)
                 tile = jnp.take_along_axis(up[i * SUB : (i + 1) * SUB, at], flip, axis=0, mode="promise_in_bounds")
-                centre[EDGE - (i + 1) * SUB : EDGE - i * SUB, at] = tile
+                centre[HALF - (i + 1) * SUB : HALF - i * SUB, at] = tile
 
     lay(times(whole(rows_c), whole(cols_a, 0)), times(whole(rows_s), whole(cols_b, 0)))
     for g in range(GROUPS):
         columns(g, 1)
+
+    def come(dr, dc):
+        @pl.when(inside(dr, dc))
+        def _():
+            slot_of = w_all.at[place(dr, dc)]
+            pltpu.make_async_copy(slot_of, slot_of, recv_w.at[place(dr, dc)]).wait()
+
+    for dr, dc in NEAR:
+        come(dr, dc)
+    for dr, dc in NEAR:
+        turn(place(dr, dc), w_all[place(dr, dc), 0], w_all[place(dr, dc), 1])
+    for g in range(GROUPS):
+        edges(g, 1)
+    strip = times(whole(edge_r), whole(plain_c, 0)) - times(whole(edge_i), whole(plain_s, 0))
+    top = rim[0] * t_own + strip[:M] * t_next
+    centre[R - M :, :] = rim[1] * t_own + strip[M:] * t_next
+    for i in range(M // SUB):
+        for k in range(WIDE // LANES):
+            at = slice(k * LANES, (k + 1) * LANES)
+            tile = jnp.take_along_axis(top[i * SUB : (i + 1) * SUB, at], flip, axis=0, mode="promise_in_bounds")
+            centre[M - (i + 1) * SUB : M - i * SUB, at] = tile
 
     for j in range(PIECES):
         @pl.when(me != REDUCERS[j])
@@ -393,15 +432,15 @@
         @pl.when(inside(dr, dc))
         def _():
             weight_copy(dr, dc).wait_send()
-            slot_of = w_all.at[place(dr, dc)]
-            pltpu.make_async_copy(slot_of, slot_of, recv_w.at[place(dr, dc)]).wait()
-
-    for dr, dc in AROUND:
+
+    for dr, dc in FAR:
+        come(dr, dc)
+    for dr, dc in FAR:
         turn(place(dr, dc), w_all[place(dr, dc), 0], w_all[place(dr, dc), 1])
 
 
 def image_kernel(
-    w_ref, wave_v, turn_v, rim_wave, rows_c, rows_s, cols_a, cols_b, plain_c, plain_s, centre, rim, out_hbm,
+    w_ref, wave_v, turn_v, rim_wave, rows_c, rows_s, cols_a, cols_b, plain_c, plain_s, centre, mid_r, mid_i, out_hbm,
     edge_a, edge_b, edge_r, edge_i, image, out_sem,
 ):
     f32, i32, bf16 = jnp.float32, jnp.int32, jnp.bfloat16
@@ -411,7 +450,7 @@
         copy.start()
         return copy
 
-    stores = [store(0, centre, (M, 2 * EDGE), (LANES, WIDE))]
+    stores = [store(0, centre, (0, R), (LANES, WIDE))]
     low = lax.broadcasted_iota(i32, (LOW, LANES), 0)
     lowf = low.astype(f32)
 
@@ -453,8 +492,8 @@
                     real, imag = w_r * c - w_i * s, w_r * s + w_i * c
                 else:
                     real, imag = w_r * c + w_i * s, w_i * c - w_r * s
-                edge_r[side, g, at : at + LOW, :] = real.astype(bf16)
-                edge_i[side, g, at : at + LOW, :] = imag.astype(bf16)
+                edge_r[side // 2, g, at : at + LOW, :] = real.astype(bf16)
+                edge_i[side // 2, g, at : at + LOW, :] = imag.astype(bf16)
 
     def whole(ref, at=None):
         return jnp.concatenate([ref[g] if at is None else ref[at, g] for g in range(GROUPS)], 1)
@@ -484,7 +523,7 @@
 
     for g in range(GROUPS):
         shared(g)
-        for side in range(3):
+        for side in (0, 2):
             edges(g, side)
 
     column = lax.broadcasted_iota(i32, (1, WIDE), 1)
@@ -493,10 +532,10 @@
     t_left = jnp.maximum(M - 0.5 - column, 0.0) * (1 / (2 * M))
     t_right = jnp.maximum(column - (C - M - 0.5), 0.0) * (1 / (2 * M))
 
-    def strips(sides, spot):
-        real = jnp.concatenate([whole(edge_r, side) for side in sides], 0)
-        imag = jnp.concatenate([whole(edge_i, side) for side in sides], 0)
-        return times(real, whole(plain_c, spot)) - times(imag, whole(plain_s, spot))
+    def strips():
+        real = jnp.concatenate([whole(edge_r, 0), whole(mid_r), whole(edge_r, 1)], 0)
+        imag = jnp.concatenate([whole(edge_i, 0), whole(mid_i), whole(edge_i, 1)], 0)
+        return times(real, whole(plain_c, 1)) - times(imag, whole(plain_s, 1))
 
     def outer_cols(inner_ref, edge_ref):
         parts = []
@@ -512,17 +551,14 @@
         at = slice(k * LANES, (k + 1) * LANES)
         lay(down[:EDGE, at], up[:EDGE, at], start)
         stores.append(store(1 + k, image.at[pl.ds(M, 2 * EDGE), pl.ds(start, LANES)], (M, 2 * EDGE), (start, LANES)))
-    strip = strips((1,), 0)
-    for k in range(2):
-        at = slice(k * LANES, (k + 1) * LANES)
-        seam(rim[0, :, at], rim[1, :, at], strip[:, at], (k + 1) * LANES)
-    strip = strips((0, 1, 2), 1)
+    strip = strips()
     strip = strip[: 2 * M] * t_left + strip[2 * M : 4 * M] * t_mid + strip[4 * M :] * t_right
     for k, start in ((0, 0), (1, C - LANES)):
         at = slice(k * LANES, (k + 1) * LANES)
         seam(up[EDGE:, at], down[EDGE:, at], strip[:, at], start)
-    for n, row in ((3, 0), (4, R - M)):
-        stores.append(store(n, image.at[pl.ds(row, M)], (row, M), (0, C)))
+    for n, row in ((3, 0), (5, R - M)):
+        for k, start in ((0, 0), (1, C - LANES)):
+            stores.append(store(n + k, image.at[pl.ds(row, M), pl.ds(start, LANES)], (row, M), (start, LANES)))
     for copy in stores:
         copy.wait()
 
@@ -542,8 +578,9 @@
         vmem((2, GROUPS, WIDE, LANES), bf16),
         vmem((2, GROUPS, WIDE, LANES), bf16),
         vmem((2, GROUPS, WIDE, LANES), bf16),
-        vmem((2 * EDGE, WIDE), f32),
-        vmem((2, M, WIDE), f32),
+        vmem((R, WIDE), f32),
+        vmem((GROUPS, 2 * M, LANES), bf16),
+        vmem((GROUPS, 2 * M, LANES), bf16),
     )
     tables = pl.pallas_call(
         exchange_kernel,
@@ -568,6 +605,7 @@
             vmem((2, SUB, LANES), i32),
             vmem((2, SUB, LANES), f32),
             vmem((2, LOW // SUB - 1, 2, SUB, LANES), f32),
+            vmem((2, M, WIDE), f32),
             dma((7,)), dma((PIECES,)), dma, dma((DEPTH,)), dma, dma((PLANE,)), dma, dma((9,)), dma((9,)),
         ],
         compiler_params=pltpu.CompilerParams(collective_id=0, has_side_effects=True, vmem_limit_bytes=24 * 1024 * 1024),
@@ -581,10 +619,10 @@
         scratch_shapes=[
             vmem((GROUPS, 2 * M, LANES), bf16),
             vmem((GROUPS, 2 * M, LANES), bf16),
-            vmem((3, GROUPS, 2 * M, LANES), bf16),
-            vmem((3, GROUPS, 2 * M, LANES), bf16),
+            vmem((2, GROUPS, 2 * M, LANES), bf16),
+            vmem((2, GROUPS, 2 * M, LANES), bf16),
             vmem((R, C), f32),
-            dma((5,)),
+            dma((7,)),
         ],
         compiler_params=pltpu.CompilerParams(vmem_limit_bytes=24 * 1024 * 1024),
         name="image",

time: 40.3 us -> 39.9 us (0.990)
  Pallas kernels: 40.2 us -> 39.7 us
where the time goes in v5:
time: 39.9 us; the launch traced here: 39.7 us
  Pallas kernels  39.7 us (99%)
    pallas_call x1, Pallas kernels, tile_of(): pl.pallas_call(exchange_kernel, out_shape=kept, in_specs=[pl.BlockSpec(me...  37.6 us
    pallas_call x1, Pallas kernels, tile_of(): pl.pallas_call(image_kernel, out_shape=jax.ShapeDtypeStruct((R, C), f32),...  2.09 us

profile of v5, /device:TPU:39, one launch (start us, length us, event | category | flops | bytes accessed | tf_op | source)
XLA Modules:
  0.0 39.7 jit_solution(10837496635047903794)
XLA Ops:
  0.0 37.6 %exchange.1 = (f32[18,8,128]{2,1,0:T(8,128)S(1)}, f32[2,8,32,128]{3,2,1,0:T(8,128)S(1)}, f32[2,8,8,128]{3,2,1,0:T(8,128)S(1)}, f32[2,8,64,128]{3,2,1,0:T(8,128)S...) custom-call(s32[512]{0:T(512)} %order_hbm.1, ...), custom_call_target="tpu_custom_call" | custom-call | tf_op jit(solution)/shard_map/exchange/pallas_call | solution.py:585
  37.6 2.1 %image.1 = f32[1024,512]{1,0:T(8,128)} custom-call(f32[18,8,128]{2,1,0:T(8,128)S(1)} %get-tuple-element.18.w_ref, f32[2,8,32,128]{3,2,1,0:T(8,128)S(1)} %get-tuple-element.19.wave_v, f32[2,8,8,128]{3,2,1,0:T(8,128)S(1)} %get-tuple-element.20.turn_v, f32[2,8,64,128]{3,2,1,0:T(8,128)S(1)} %get-tuple-element.21.rim_wave, ...), custom_call_target="tpu_custom_call" | custom-call | tf_op jit(solution)/shard_map/image/pallas_call | solution.py:614

commit v6 on v5

--- a/solution.py
+++ b/solution.py
@@ -67,7 +67,7 @@
 def exchange_kernel(
     order_hbm, vis_hbm, pairs_hbm, slot_hbm, ucell_hbm, vcell_hbm, gain_hbm,
     w_ref, wave_v, turn_v, rim_wave, rows_c, rows_s, cols_a, cols_b, plain_c, plain_s, centre, edge_r, edge_i,
-    order, vis, pairs, slot, ucell, vcell, gain, pay, raw, part, line, done, w_own, w_all, uv_ref, turn_u, spin, rim,
+    order, vis, pairs, slot, ucell, vcell, gain, pay, raw, part, line, done, w_own, w_all, uv_ref, turn_u, spin, rim, sent,
     in_sem, send1, recv1, send2, recv2, send3, recv3, send_w, recv_w,
 ):
     fr, fc = lax.axis_index("frow"), lax.axis_index("fcol")
@@ -145,19 +145,19 @@
 
     def piece_copy(j):
         return pltpu.make_async_remote_copy(
-            src_ref=pay.at[j], dst_ref=raw.at[me], send_sem=send1.at[j], recv_sem=recv1,
+            src_ref=pay.at[j], dst_ref=raw.at[me], send_sem=send1, recv_sem=recv1,
             device_id=in_plane(REDUCERS[j]), device_id_type=MESH,
         )
 
     def line_copy(z):
         return pltpu.make_async_remote_copy(
-            src_ref=part, dst_ref=line.at[my_z], send_sem=send2.at[z], recv_sem=recv2,
+            src_ref=part, dst_ref=line.at[my_z], send_sem=send2, recv_sem=recv2,
             device_id=in_line(z), device_id_type=MESH,
         )
 
     def done_copy(s):
         return pltpu.make_async_remote_copy(
-            src_ref=done.at[mine], dst_ref=done.at[mine], send_sem=send3.at[s], recv_sem=recv3,
+            src_ref=done.at[mine], dst_ref=done.at[mine], send_sem=send3, recv_sem=recv3,
             device_id=in_plane(s), device_id_type=MESH,
         )
 
@@ -411,22 +411,15 @@
             tile = jnp.take_along_axis(top[i * SUB : (i + 1) * SUB, at], flip, axis=0, mode="promise_in_bounds")
             centre[M - (i + 1) * SUB : M - i * SUB, at] = tile
 
-    for j in range(PIECES):
-        @pl.when(me != REDUCERS[j])
-        def _():
-            piece_copy(j).wait_send()
-
     @pl.when(reduces)
     def _():
-        for z in range(DEPTH):
-            @pl.when(my_z != z)
-            def _():
-                line_copy(z).wait_send()
-
-        for s in range(PLANE):
-            @pl.when(me != s)
-            def _():
-                done_copy(s).wait_send()
+        landed(pay, PIECES - 1, send1)
+        landed(line, DEPTH - 1, send2)
+        landed(sent, PLANE - 1, send3)
+
+    @pl.when(jnp.logical_not(reduces))
+    def _():
+        landed(pay, PIECES, send1)
 
     for dr, dc in AROUND:
         @pl.when(inside(dr, dc))
@@ -606,7 +599,8 @@
             vmem((2, SUB, LANES), f32),
             vmem((2, LOW // SUB - 1, 2, SUB, LANES), f32),
             vmem((2, M, WIDE), f32),
-            dma((7,)), dma((PIECES,)), dma, dma((DEPTH,)), dma, dma((PLANE,)), dma, dma((9,)), dma((9,)),
+            vmem((PLANE - 1, NBLK, LANES), f32),
+            dma((7,)), dma, dma, dma, dma, dma, dma, dma((9,)), dma((9,)),
         ],
         compiler_params=pltpu.CompilerParams(collective_id=0, has_side_effects=True, vmem_limit_bytes=24 * 1024 * 1024),
         name="exchange",

time: 39.9 us -> 39.4 us (0.987)
  Pallas kernels: 39.7 us -> 39.2 us
    pallas_call x1, Pallas kernels: 37.6 us -> 37.1 us  [tile_of(): pl.pallas_call(exchange_kernel, out_shape=kept, in_specs=[pl.BlockSpec(me...]
where the time goes in v6:
time: 39.4 us; the launch traced here: 39.2 us
  Pallas kernels  39.2 us (99%)
    pallas_call x1, Pallas kernels, tile_of(): pl.pallas_call(exchange_kernel, out_shape=kept, in_specs=[pl.BlockSpec(me...  37.1 us
    pallas_call x1, Pallas kernels, tile_of(): pl.pallas_call(image_kernel, out_shape=jax.ShapeDtypeStruct((R, C), f32),...  2.09 us

profile of v6, /device:TPU:39, one launch (start us, length us, event | category | flops | bytes accessed | tf_op | source)
XLA Modules:
  0.0 39.2 jit_solution(4410986159877818537)
XLA Ops:
  0.0 37.1 %exchange.1 = (f32[18,8,128]{2,1,0:T(8,128)S(1)}, f32[2,8,32,128]{3,2,1,0:T(8,128)S(1)}, f32[2,8,8,128]{3,2,1,0:T(8,128)S(1)}, f32[2,8,64,128]{3,2,1,0:T(8,128)S...) custom-call(s32[512]{0:T(512)} %order_hbm.1, ...), custom_call_target="tpu_custom_call" | custom-call | tf_op jit(solution)/shard_map/exchange/pallas_call | solution.py:578
  37.1 2.1 %image.1 = f32[1024,512]{1,0:T(8,128)} custom-call(f32[18,8,128]{2,1,0:T(8,128)S(1)} %get-tuple-element.18.w_ref, f32[2,8,32,128]{3,2,1,0:T(8,128)S(1)} %get-tuple-element.19.wave_v, f32[2,8,8,128]{3,2,1,0:T(8,128)S(1)} %get-tuple-element.20.turn_v, f32[2,8,64,128]{3,2,1,0:T(8,128)S(1)} %get-tuple-element.21.rim_wave, ...), custom_call_target="tpu_custom_call" | custom-call | tf_op jit(solution)/shard_map/image/pallas_call | solution.py:608
